TPU v7x, 32 devices: a whole 2x2x4 slice. The times are simulated.
32 devices in a mesh: dp: 4 (over y, x), seq: 8 (over z, core).
Axes of the slice: x: 2, y: 2, z: 4, core: 2. Of those that a mesh axis runs over, the one named last changes fastest.
Arguments:
- tokens: bfloat16 [4, 2048, 2560], P('dp', 'seq'), may hold values from -6 to 6
- values: bfloat16 [4, 2048, 5120], P('dp', 'seq'), may hold values from -6 to 6
- out_grad: bfloat16 [4, 2048, 5120], P('dp', 'seq'), may hold values from -0.0029296875 to 0.0029296875
- w_bc: bfloat16 [2560, 256], replicated, may hold values from -0.009765625 to 0.009765625
- w_dt: bfloat16 [2560, 80], replicated, may hold values from -0.125 to 0.125
- a_log: float32 [80], replicated, may hold values from -13 to -2
- dt_bias: float32 [80], replicated, may hold values from -1 to 1
- fire_flags: int32 [4], P('dp'), may hold values from 0 to 1, as said below
- last_bc: float32 [4, 2560, 256], P('dp', 'seq'), may hold values from -27 to 27
- last_heads: float32 [4, 2, 80], P('dp'), may hold values from -6 to 6
- total_bc: float32 [2560, 256], P('seq'), may hold values from -6 to 6
- total_heads: float32 [2, 80], replicated, may hold values from -6 to 6
Outputs:
- new_total_bc: float32 [2560, 256], P('seq')
- new_total_heads: float32 [2, 80], replicated
- new_last_bc: float32 [4, 2560, 256], P('dp', 'seq')
- new_last_heads: float32 [4, 2, 80], P('dp')
- trigger: float32 [4], P('dp')
Inputs may be any that keep to these rules, and one draw needn't show every extreme that they name: `fire_flags`: between 2 and 3 entries are 1; which ones varies.
All inputs are finite; a program needn't handle non-finite values.
Results may differ from a plain program's by a relative error of at most 0.0029.
Values sent between devices are 32-bit elements; how exact they have to be, the bound alone decides.
A program may use at most 320 MiB of HBM per device.

v0:
```python
import jax
import jax.numpy as jnp
from jax import lax
from jax.sharding import PartitionSpec as P

GROUP = 128


HIGHEST = lax.Precision.HIGHEST


def prefix(part, axis, combine, identity, reverse):
    count = lax.axis_size(axis)
    place = lax.axis_index(axis)
    ahead = count - 1 - place if reverse else place
    gathered = jax.tree.map(lambda a: lax.all_gather(a, axis), part)
    state = jax.tree.map(lambda a, e: jnp.zeros_like(a) + jnp.asarray(e, a.dtype), part, identity)

    def one(turn, state):
        source = count - 1 - turn if reverse else turn
        return combine(
            state, jax.tree.map(lambda a: lax.dynamic_index_in_dim(a, source, 0, False), gathered)
        )

    return lax.fori_loop(0, ahead, one, state)


def project_heads(projected, raw_dt, a_log, dt_bias):
    half_width = projected.shape[1] // 2
    step_rates = jax.nn.softplus(raw_dt + dt_bias)
    log_decay = -step_rates * jnp.exp(a_log)
    return (projected[:, :half_width], projected[:, half_width:], step_rates, log_decay)


def group_terms(carried, pieces):
    state_now, loss_sum = carried
    value_rows, b_rows, c_rows, step_rates, log_decay, grad_rows = pieces
    block_len, head_count = step_rates.shape
    values_full = value_rows.astype(jnp.float32).reshape(block_len, head_count, -1)
    grads_full = grad_rows.astype(jnp.float32).reshape(block_len, head_count, -1)
    cumulated = jnp.cumsum(log_decay, axis=0)
    decay_gap = cumulated.T[:, :, None] - cumulated.T[:, None, :]
    causal = lax.broadcasted_iota(jnp.int32, (block_len, block_len), 0) >= lax.broadcasted_iota(
        jnp.int32, (block_len, block_len), 1
    )
    decay_mat = jnp.exp(jnp.where(causal[None], decay_gap, -1e30))
    scores = jnp.dot(c_rows, b_rows.T, precision=HIGHEST)
    mix_weights = decay_mat * scores[None] * step_rates.T[:, None, :]
    inside = jnp.einsum("hts,shp->thp", mix_weights, values_full, precision=HIGHEST)
    outside = (
        jnp.einsum("tn,hnp->thp", c_rows, state_now, precision=HIGHEST)
        * jnp.exp(cumulated)[:, :, None]
    )
    loss_sum = loss_sum + jnp.sum((inside + outside) * grads_full)
    tail_weight = jnp.exp(cumulated[-1] - cumulated) * step_rates
    fresh = jnp.einsum(
        "sn,shp->hnp", b_rows, tail_weight[:, :, None] * values_full, precision=HIGHEST
    )
    state_now = jnp.exp(cumulated[-1])[:, None, None] * state_now + fresh
    return ((state_now, loss_sum), None)


def in_blocks(array):
    blocks = array.shape[0] // GROUP
    return array.reshape((blocks, GROUP) + array.shape[1:])


def sequence_loss(state_start, value_rows, b_rows, c_rows, step_rates, log_decay, grad_rows):
    pieces = (
        in_blocks(value_rows),
        in_blocks(b_rows),
        in_blocks(c_rows),
        in_blocks(step_rates),
        in_blocks(log_decay),
        in_blocks(grad_rows),
    )
    carried, unused = lax.scan(
        jax.checkpoint(group_terms), (state_start, jnp.zeros((), jnp.float32)), pieces
    )
    return carried[1]


def block_summary(projected, raw_dt, value_rows, a_log, dt_bias):
    b_rows, c_rows, step_rates, log_decay = project_heads(projected, raw_dt, a_log, dt_bias)
    block_len, head_count = step_rates.shape
    values_full = value_rows.astype(jnp.float32).reshape(block_len, head_count, -1)
    cumulated = jnp.cumsum(log_decay, axis=0)
    tail_weight = jnp.exp(cumulated[-1] - cumulated) * step_rates
    fresh = jnp.einsum(
        "sn,shp->hnp", b_rows, tail_weight[:, :, None] * values_full, precision=HIGHEST
    )
    return (jnp.exp(cumulated[-1]), fresh)


def combine_states(earlier, later):
    return (earlier[0] * later[0], later[0][:, None, None] * earlier[1] + later[1])


def local(
    tokens,
    values,
    out_grad,
    w_bc,
    w_dt,
    a_log,
    dt_bias,
    fire_flags,
    last_bc,
    last_heads,
    total_bc,
    total_heads,
):
    tok_rows = tokens[0]
    value_rows = values[0]
    grad_rows = out_grad[0]
    projected = jnp.dot(tok_rows, w_bc, preferred_element_type=jnp.float32)
    raw_dt = jnp.dot(tok_rows, w_dt, preferred_element_type=jnp.float32)

    def summary_of(projected, a_log, dt_bias):
        return block_summary(projected, raw_dt, value_rows, a_log, dt_bias)

    (decay_total, fresh), pull_summary = jax.vjp(summary_of, projected, a_log, dt_bias)
    b_rows, c_rows, step_rates, log_decay = project_heads(projected, raw_dt, a_log, dt_bias)
    block_len, head_count = log_decay.shape
    cumulated = jnp.cumsum(log_decay, axis=0)
    grads_full = grad_rows.astype(jnp.float32).reshape(block_len, head_count, -1)
    entry = jnp.einsum(
        "tn,thp->hnp", c_rows, jnp.exp(cumulated)[:, :, None] * grads_full, precision=HIGHEST
    )
    identity = (jnp.ones_like(decay_total), jnp.zeros_like(fresh))
    state_in = prefix((decay_total, fresh), "seq", combine_states, identity, False)[1]
    state_back = prefix((decay_total, entry), "seq", combine_states, identity, True)[1]

    def loss_of(projected, a_log, dt_bias):
        b_part, c_part, rate_part, decay_part = project_heads(projected, raw_dt, a_log, dt_bias)
        return sequence_loss(state_in, value_rows, b_part, c_part, rate_part, decay_part, grad_rows)

    loss_here, pull_loss = jax.vjp(loss_of, projected, a_log, dt_bias)
    loss_proj, loss_alog, loss_bias = pull_loss(jnp.ones_like(loss_here))
    link_decay = jnp.sum(state_back * state_in, axis=(1, 2))
    link_proj, link_alog, link_bias = pull_summary((link_decay, state_back))
    grad_bc = jnp.einsum(
        "td,tk->dk",
        tok_rows,
        (loss_proj + link_proj).astype(jnp.bfloat16),
        preferred_element_type=jnp.float32,
    )
    grad_heads = jnp.stack([loss_alog + link_alog, loss_bias + link_bias])
    own_last = last_bc[0]
    own_rows = lax.psum_scatter(grad_bc, "seq", scatter_dimension=0, tiled=True)
    diff_bc = own_rows - own_last
    square_bc, summed_heads = lax.psum((jnp.sum(diff_bc * diff_bc), grad_heads), "seq")
    diff_heads = summed_heads - last_heads[0]
    trigger = jnp.sqrt(square_bc + jnp.sum(diff_heads * diff_heads) + 1e-06)
    weight = fire_flags[0].astype(jnp.float32)
    fired_bc, fired_heads = lax.psum((weight * diff_bc, weight * diff_heads), "dp")
    new_total_bc = total_bc + fired_bc
    new_total_heads = total_heads + fired_heads
    new_last_bc = jnp.where(fire_flags[0] > 0, own_rows, own_last)[None]
    new_last_heads = jnp.where(fire_flags[0] > 0, summed_heads, last_heads[0])[None]
    return (new_total_bc, new_total_heads, new_last_bc, new_last_heads, trigger.reshape(1))


def solution(mesh):
    in_specs = (
        P("dp", "seq", None),
        P("dp", "seq", None),
        P("dp", "seq", None),
        P(),
        P(),
        P(),
        P(),
        P("dp"),
        P("dp", "seq", None),
        P("dp", None, None),
        P("seq", None),
        P(),
    )
    out_specs = (P("seq", None), P(), P("dp", "seq", None), P("dp", None, None), P("dp"))
    return jax.shard_map(local, mesh=mesh, in_specs=in_specs, out_specs=out_specs, check_vma=False)
```

profile of v0, /device:TPU:0, one launch (start us, length us, event | category | flops | bytes accessed | tf_op | source)
XLA Modules:
  0.0 909.3 jit_solution(7935674866625949734)
XLA Ops:
  11.7 4.4 copy.251
  16.1 7.5 fusion.57
  24.5 4.4 copy.238
  28.9 4.8 convert.3
  34.0 14.1 %all-gather.2 = f32[8,1,80]{2,1,0:T(1,128)S(1)} all-gather(f32[1,1,80]{2,1,0:T(1,128)S(1)} %bitcast.420), channel_id=1, replica_groups=mesh['dp'=4,'seq'=8] {'seq'}, dimensions={0}, use_global_device_ids=true | all-gather | bytes 2880 | tf_op jit(solution)/shard_map/all_gather | solution.py:16
  48.1 163.8 %all-gather.8.cloned.1.call-done = f32[640,128,64]{1,2,0:T(8,128)} async-done(((f32[80,128,64]{1,2,0:T(8,128)}), f32[640,128,64]{1,2,0:T(8,128)}) %all-gather.8.cloned.1.call-update) | async-done | bytes 20971536 | tf_op jit(solution)/shard_map/all_gather | solution.py:16
  214.8 110.1 %while.65 = (s32[]{:T(128)}, f32[80,128,64]{2,1,0:T(8,128)}, s32[]{:T(128)}, f32[8,80]{1,0:T(8,128)S(1)}, f32[8,80,128,64]{2,3,1,0:T(8,128)}, /*index=5*/s32[]{:T(128)}, s32[]{:T(128)}, s32[]{:T(128)}, s32[]{:T(128)}) while((s32[]{:T(128)}, f32[80,128,64]{2,1,0:T(8,128)}, s32[]{:T(128)}, f32[8,80]{1,0:T(8,128)S(1)}, ...), condition=%wide.region_22.24_spmd, body=%wide.region_21.23_spmd.sunk | while | flops 1310726 | bytes 18351188 | solution.py:25
  218.4 5.2 copy.364
  223.6 6.9 bitcast_add_fusion.14
  234.0 5.2 copy.364
  239.3 6.9 bitcast_add_fusion.14
  249.7 5.2 copy.364
  254.9 6.9 bitcast_add_fusion.14
  265.4 5.2 copy.364
  270.6 6.9 bitcast_add_fusion.14
  281.0 5.2 copy.364
  286.3 6.9 bitcast_add_fusion.14
  296.7 5.2 copy.364
  302.0 6.9 bitcast_add_fusion.14
  312.4 5.2 copy.364
  317.6 6.9 bitcast_add_fusion.14
  325.0 5.7 copy.258
  330.6 9.8 %fusion.44 = f32[256,80]{0,1:T(8,128)S(1)} fusion(f32[256,80,64]{0,2,1:T(8,128)} %convert.3, f32[80,64,128]{2,0,1:T(8,128)} %copy.258, f32[256,256]{1,0:T(8,128)S(1)} %fusion.59), kind=kOutput, calls=%fused_computation.78 | convolution fusion | flops 2015866880 | bytes 8077312 | tf_op jit(solution)/shard_map/transpose(jvp(sn,shp->hnp))/dot_general | solution.py:89
  341.9 5.7 fusion.54
  348.0 4.4 copy.243
  352.4 20.1 %fusion.63 = f32[256,128]{1,0:T(8,128)} fusion(bf16[256,80,64]{0,2,1:T(8,128)(2,1)} %bitcast.399, f32[256,80]{0,1:T(8,128)S(1)} %get-tuple-element.835, f32[80,128,64]{2,1,0:T(8,128)} %get-tuple-element.468), kind=kOutput, calls=%fused_computation.97 | convolution fusion | flops 2015887360 | bytes 5455872 | tf_op jit(solution)/shard_map/transpose(jvp(sn,shp->hnp))/dot_general | solution.py:89
  372.5 158.8 %all-gather.6.cloned.1.call-done = f32[640,128,64]{1,2,0:T(8,128)} async-done(((f32[80,128,64]{1,2,0:T(8,128)}), f32[640,128,64]{1,2,0:T(8,128)}) %all-gather.6.cloned.1.call-update) | async-done | bytes 20971536 | tf_op jit(solution)/shard_map/all_gather | solution.py:16
  534.3 5.5 copy.240
  539.8 20.7 %while.64 = (s32[]{:T(128)}, f32[80,128,64]{1,2,0:T(8,128)}, f32[2,80,128,64]{2,3,1,0:T(8,128)}, f32[2,128,80]{2,1,0:T(8,128)S(1)}, f32[2,128,80]{1,0,2:T(2,128)...) while((s32[]{:T(128)}, f32[80,128,64]{1,2,0:T(8,128)}, ...), condition=%wide.region_6.8_spmd, body=%wide.region_4.7_spmd.sunk | while | flops 1010575360 | bytes 17681072 | solution.py:77
  545.3 4.8 bitcast_add_fusion.13
  555.7 4.8 bitcast_add_fusion.13
  563.1 138.3 %while.66 = (s32[]{:T(128)}, f32[80,128,64]{1,2,0:T(8,128)}, f32[]{:T(128)}, f32[2,128,128]{2,1,0:T(8,128)}, f32[2,128,128]{2,1,0:T(8,128)}, /*index=5*/f32[2,12...) while((s32[]{:T(128)}, f32[80,128,64]{1,2,0:T(8,128)}, ...), condition=%wide.region_18.20_spmd.clone, body=%wide.region_7.19_spmd.clone.sunk | while | flops 6145556480 | bytes 128295160 | solution.py:77
  591.7 5.0 fusion.172
  601.8 9.5 %fusion.170 = (f32[80,128]{1,0:T(8,128)S(1)}, f32[80,128]{1,0:T(8,128)S(1)}, f32[80,128]{1,0:T(8,128)S(1)}, f32[128,128]{1,0:T(8,128)S(1)}) fusion(f32[128,128]{1,0:T(8,128)S(1)} %fusion.169, f32[80,128]{1,0:T(8,128)S(1)} %bitcast.409, f32[80,128]{1,0:T(8,128)S(1)} %copy.372, pred[128,128]{1,0:T(8,128)(4,1)S(1)} %iota_compare_fusion.2, ...), kind=kOutput, calls=%fused_computation.24.clone.1 | convolution fusion | flops 1023625216 | bytes 4284416 | tf_op jit(solution)/shard_map/transpose(jvp())/while/body/eval_jaxpr/checkpoint/hts,shp->thp/dot_general | solution.py:49
  611.6 8.6 fusion.171
  620.3 4.4 fusion.177
  625.0 6.8 fusion.175
  649.1 5.0 fusion.172
  659.2 9.5 %fusion.170 = (f32[80,128]{1,0:T(8,128)S(1)}, f32[80,128]{1,0:T(8,128)S(1)}, f32[80,128]{1,0:T(8,128)S(1)}, f32[128,128]{1,0:T(8,128)S(1)}) fusion(f32[128,128]{1,0:T(8,128)S(1)} %fusion.169, f32[80,128]{1,0:T(8,128)S(1)} %bitcast.409, f32[80,128]{1,0:T(8,128)S(1)} %copy.372, pred[128,128]{1,0:T(8,128)(4,1)S(1)} %iota_compare_fusion.2, ...), kind=kOutput, calls=%fused_computation.24.clone.1 | convolution fusion | flops 1023625216 | bytes 4284416 | tf_op jit(solution)/shard_map/transpose(jvp())/while/body/eval_jaxpr/checkpoint/hts,shp->thp/dot_general | solution.py:49
  669.1 8.6 fusion.171
  677.8 4.4 fusion.177
  682.4 6.8 fusion.175
  690.3 3.9 bitcast_add_fusion.15
  709.3 5.0 multiply_reduce_fusion.3
  717.8 135.8 %reduce-scatter.4.cloned.1.call-done = f32[320,256]{1,0:T(8,128)} async-done(((f32[2560,256]{1,0:T(8,128)}), f32[320,256]{1,0:T(8,128)}) %reduce-scatter.4.cloned.1.call-update) | async-done | bytes 327696
  856.2 15.7 %all-reduce.7 = (f32[2,80]{1,0:T(2,128)S(1)}, f32[]{:T(128)}) all-reduce(f32[2,80]{1,0:T(2,128)S(1)} %pad_maximum_fusion, f32[]{:T(128)} %get-tuple-element.831), channel_id=1, replica_groups=mesh['dp'=4,'seq'=8] {'seq'}, use_global_device_ids=true, to_apply=%region_34.36 | all-reduce | flops 161 | bytes 1288 | tf_op jit(solution)/shard_map/psum | solution.py:152
  875.2 9.9 %psum.30 = f32[2,80]{1,0:T(2,128)S(1)} all-reduce(f32[2,80]{1,0:T(2,128)S(1)} %get-tuple-element.839), channel_id=1, replica_groups=mesh['dp'=4,'seq'=8] {'dp'}, use_global_device_ids=true, to_apply=%region_35.37 | all-reduce | flops 160 | bytes 1280 | tf_op jit(solution)/shard_map/psum | solution.py:156
  885.7 13.9 %all-reduce.10.cloned.1.call-done = f32[320,256]{0,1:T(8,128)} async-done(((f32[320,256]{0,1:T(8,128)}), f32[320,256]{0,1:T(8,128)}) %all-reduce.10.cloned.1.call-update) | async-done | bytes 327696 | tf_op jit(solution)/shard_map/psum | solution.py:156
  (273 shorter events, 109.2 us)
Async XLA Ops:
  7.2 204.7 %all-gather.8.cloned.1.call-start = ((), (), s32[]{:S(2)}) async-start(), calls=%async_computation.3 | async-start | bytes 23592960 | tf_op jit(solution)/shard_map/all_gather | solution.py:16
  10.1 330.4 %copy-start.13 = (f32[256,80]{0,1:T(8,128)}, f32[256,80]{0,1:T(8,128)S(1)}, u32[]{:S(2)}) copy-start(f32[256,80]{0,1:T(8,128)S(1)} %get-tuple-element.841) | copy-start | bytes 245764
  23.5 507.8 %all-gather.6.cloned.1.call-start = ((), (), s32[]{:S(2)}) async-start(), calls=%async_computation.2 | async-start | bytes 23592960 | tf_op jit(solution)/shard_map/all_gather | solution.py:16
  24.2 316.2 %copy-start.8 = (f32[80,2,128]{2,0,1:T(8,128)}, f32[80,2,128]{2,0,1:T(8,128)S(1)}, u32[]{:S(2)}) copy-start(f32[80,2,128]{2,0,1:T(8,128)S(1)} %reduce-window.20) | copy-start | bytes 245764
  24.5 316.0 %copy-start.34 = (f32[80,2]{0,1:T(2,128)}, f32[80,2]{0,1:T(2,128)S(1)}, u32[]{:S(2)}) copy-start(f32[80,2]{0,1:T(2,128)S(1)} %slice.45) | copy-start | bytes 1924
  33.8 181.0 %copy-start.26 = (f32[256,80]{0,1:T(8,128)}, f32[256,80]{0,1:T(8,128)S(1)}, u32[]{:S(2)}) copy-start(f32[256,80]{0,1:T(8,128)S(1)} %bitcast_bitcast_fusion.2) | copy-start | bytes 245764
  34.0 306.5 %copy-start.38 = (f32[80]{0:T(128)}, f32[80]{0:T(128)S(1)}, u32[]{:S(2)}) copy-start(f32[80]{0:T(128)S(1)} %get-tuple-element.753) | copy-start | bytes 964
  330.6 11.2 %copy-start.7 = (bf16[1,256,5120]{1,2,0:T(8,128)(2,1)S(1)}, bf16[1,256,5120]{1,2,0:T(8,128)(2,1)}, u32[]{:S(2)}) copy-start(bf16[1,256,5120]{1,2,0:T(8,128)(2,1)} %copy.238) | copy-start | bytes 7864324
  340.4 7.1 copy-start.15
  347.6 506.0 %reduce-scatter.4.cloned.1.call-start = ((), (), s32[]{:S(2)}) async-start(), calls=%async_computation.4 | async-start | bytes 2949120
  591.6 5.7 copy-start.1
  591.6 5.0 copy-start.4
  601.8 9.5 %copy-start.32 = (f32[80]{0:T(128)S(1)}, f32[80]{0:T(128)}, u32[]{:S(2)}) copy-start(f32[80]{0:T(128)} %get-tuple-element.1072) | copy-start | bytes 964 | tf_op jit(solution)/shard_map/transpose(jvp())/while
  611.6 8.7 copy-start.3
  611.6 8.7 copy-start.5
  620.3 4.6 copy-start.2
  624.7 7.1 copy-start.17
  624.7 8.1 copy-start.33
  625.0 7.2 copy-start.20
  632.8 5.1 copy-start.21
  632.8 5.1 copy-start.28
  632.8 7.4 copy-start.11
  649.1 5.7 copy-start.1
  649.1 5.0 copy-start.4
  659.2 9.5 %copy-start.32 = (f32[80]{0:T(128)S(1)}, f32[80]{0:T(128)}, u32[]{:S(2)}) copy-start(f32[80]{0:T(128)} %get-tuple-element.1072) | copy-start | bytes 964 | tf_op jit(solution)/shard_map/transpose(jvp())/while
  669.0 8.7 copy-start.3
  669.0 8.7 copy-start.5
  677.8 4.6 copy-start.2
  682.2 7.1 copy-start.17
  682.2 8.1 copy-start.33
  682.4 7.2 copy-start.20
  690.3 5.1 copy-start.21
  690.3 5.1 copy-start.28
  690.3 7.4 copy-start.11
  707.8 191.8 %all-reduce.10.cloned.1.call-start = ((), (), s32[]{:S(2)}) async-start(), calls=%async_computation.1 | async-start | bytes 786432 | tf_op jit(solution)/shard_map/psum | solution.py:156
  709.2 5.2 copy-start.27
  709.2 5.3 copy-start.31
  709.2 8.1 copy-start.23
  709.2 8.2 copy-start.9
  709.2 8.2 copy-start.14
  709.2 8.2 copy-start.16
  709.2 8.2 copy-start.30
  709.2 8.2 copy-start.35
  709.2 8.2 copy-start.37
  709.3 8.2 copy-start.39
  709.3 8.5 copy-start.43
  714.3 157.6 %copy-start.42 = (f32[1,2,80]{2,1,0:T(2,128)S(1)}, f32[1,2,80]{2,1,0:T(2,128)}, u32[]{:S(2)}) copy-start(f32[1,2,80]{2,1,0:T(2,128)} %param.30) | copy-start | bytes 1924
  714.3 170.9 %copy-start.41 = (f32[2,80]{1,0:T(2,128)S(1)}, f32[2,80]{1,0:T(2,128)}, u32[]{:S(2)}) copy-start(f32[2,80]{1,0:T(2,128)} %param.32) | copy-start | bytes 1924
  (18 other events, 39.4 us)
Sparse Core Ops, SparseCore 0:
  23.6 188.2 all-gather.7
  347.7 183.5 all-gather.5
  707.9 145.6 reduce-scatter.3
  856.4 43.1 all-reduce.9
where the time goes:
time: 917 us; the launch traced here: 909 us
  waiting for transfers between devices  472 us (51%)
  matrix products  136 us (15%)
  local copies, waits for them, and re-layouts  132 us (14%)
  other arithmetic  85.7 us (9%)
  blocking collectives  39.6 us (4%)
  loops' own time  26.4 us (3%)
  between operations  17.6 us (2%)
    all_gather x2, waiting for transfers between devices, prefix(): gathered = jax.tree.map(lambda a: lax.all_gather(a, axis), part)  323 us
    unnamed x5, waiting for transfers between devices  136 us
    dynamic_slice x14, local copies, waits for them, and re-layouts, one(): lax.dynamic_index_in_dim(a, source, 0, False)  61.5 us
    add x7, other arithmetic, combine_states(): later[0][:, None, None] * earlier[1] + later[1]  48.2 us
    dot_general x3, matrix products, block_summary(): jnp.einsum('sn,shp->hnp', b_rows, tail_weight[:, :, None] * values_full,...  35.6 us
    dot_general x6, matrix products, group_terms(): jnp.einsum('tn,hnp->thp', c_rows, state_now, precision=HIGHEST)  33.7 us
    dot_general x6, matrix products, group_terms(): jnp.einsum('sn,shp->hnp', b_rows, tail_weight[:, :, None] * values_full,...  33.2 us
    another operation x2, loops' own time, sequence_loss(): lax.scan(jax.checkpoint(group_terms), (state_start, jnp.zeros((), jnp.flo...  25.9 us
  transfers between devices with their start and end apart: 4, of which 4 were waited for; matrix products, arithmetic and copies ran while one was open for 5% of the time, Pallas kernels for 0%

commit v1 on v0

v1 whole, which is shorter than its diff:
```python
import functools

import jax
import jax.numpy as jnp
from jax import lax
from jax.experimental import pallas as pl
from jax.experimental.pallas import tpu as pltpu
from jax.sharding import PartitionSpec as P

GROUP = 128
LANES = 256
F32 = jnp.float32
BF16 = jnp.bfloat16
HIGHEST = lax.Precision.HIGHEST
MM = (((1,), (0,)), ((), ()))
NT = (((1,), (1,)), ((), ()))
TN = (((0,), (0,)), ((), ()))


def mm(a, b, dims=MM):
    return lax.dot_general(a, b, dims, preferred_element_type=F32)


def exact(a, b, dims=MM):
    return lax.dot_general(a, b, dims, precision=HIGHEST, preferred_element_type=F32)


def halves(x):
    hi = x.astype(BF16)
    return hi, (x - hi.astype(F32)).astype(BF16)


def mm3(a, b, dims=MM):
    return mm(a[0], b[0], dims) + (mm(a[0], b[1], dims) + mm(a[1], b[0], dims))


def spread(heads, lanes, per_head, first):
    row = lax.broadcasted_iota(jnp.int32, (heads, lanes), 0)
    lane = lax.broadcasted_iota(jnp.int32, (heads, lanes), 1)
    return (row == first + lane // per_head).astype(F32).astype(BF16)


def gathers(heads, lanes, per_head, first):
    lane = lax.broadcasted_iota(jnp.int32, (lanes, heads), 0)
    row = lax.broadcasted_iota(jnp.int32, (lanes, heads), 1)
    return (row == first + lane // per_head).astype(F32).astype(BF16)


def front_kernel(
    width, tok_ref, wbc_ref, wdt_ref, alog_ref, bias_ref, x_ref, g_ref,
    fresh_ref, entry_ref, proj_ref, cum_ref, rate_ref, sigcum_ref, sig_ref, dproj_ref, ra_ref, rb_ref,
    whi, wlo, cols, rows, score, dscore,
):
    k = pl.program_id(0)
    length, heads = cum_ref.shape
    half = proj_ref.shape[1] // 2
    blocks = length // GROUP
    pairs = [(i, j) for i in range(blocks) for j in range(i + 1)]

    @pl.when(k == 0)
    def _():
        tok = tok_ref[...]
        proj = mm(tok, wbc_ref[...])
        proj_ref[...] = proj
        z = mm(tok, wdt_ref[...]) + bias_ref[...]
        tail = jnp.exp(-jnp.abs(z))
        rate = jnp.maximum(z, 0.0) + jnp.log1p(tail)
        sig = jnp.where(z >= 0, 1.0, tail) / (1.0 + tail)
        speed = jnp.exp(alog_ref[...])
        tri = (
            lax.broadcasted_iota(jnp.int32, (length, length), 0)
            >= lax.broadcasted_iota(jnp.int32, (length, length), 1)
        ).astype(F32)
        cum = exact(tri, -rate * speed)
        sigcum = exact(tri, -sig * speed)
        cum_ref[...] = cum
        rate_ref[...] = rate
        sig_ref[...] = sig
        sigcum_ref[...] = sigcum
        for n, w in enumerate((jnp.exp(cum), jnp.exp(cum[length - 1 :] - cum) * rate)):
            hi, lo = halves(w)
            whi[n] = hi
            wlo[n] = lo
        hi, lo = halves(cum)
        cols[0] = hi
        cols[1] = lo
        cols[2] = (cum - hi.astype(F32) - lo.astype(F32)).astype(BF16)
        hi, lo = halves(sigcum)
        cols[3] = hi
        cols[4] = lo
        for n, w in enumerate((cum, rate, sigcum, sig)):
            rows[n] = w.T
        b, c = proj[:, :half], proj[:, half:]
        for n, (i, j) in enumerate(pairs):
            score[n] = exact(
                c[i * GROUP : (i + 1) * GROUP], b[j * GROUP : (j + 1) * GROUP], NT
            )
        dscore[...] = jnp.zeros_like(dscore)

    lanes = x_ref.shape[1]
    group = lanes // width
    first = k * group
    xs = x_ref[...]
    gs = g_ref[...]
    hot = spread(heads, lanes, width, first)
    grow = mm(whi[0], hot) + mm(wlo[0], hot)
    fade = mm(whi[1], hot) + mm(wlo[1], hot)
    proj = proj_ref[...]
    fresh_ref[0] = mm3(halves(proj[:, :half]), halves(fade * xs.astype(F32)), TN)
    entry_ref[0] = mm3(halves(proj[:, half:]), halves(grow * gs.astype(F32)), TN)
    causal = lax.broadcasted_iota(jnp.int32, (GROUP, GROUP), 0) >= lax.broadcasted_iota(
        jnp.int32, (GROUP, GROUP), 1
    )
    lane_head = lax.broadcasted_iota(jnp.int32, (GROUP, lanes), 1) // width
    for one in range(group):
        head = first + one
        pick = spread(heads, GROUP, GROUP, head)
        cum_col = mm(cols[0], pick) + (mm(cols[1], pick) + mm(cols[2], pick))
        sig_col = mm(cols[3], pick) + mm(cols[4], pick)
        at = pl.ds(head, 1)
        cum_row, rate_row, sc_row, sig_row = (rows[n, at, :] for n in range(4))
        ra = jnp.zeros((1, GROUP), F32)
        rb = jnp.zeros((1, GROUP), F32)
        lo_lane = (one * width) // GROUP * GROUP
        span = max(GROUP, width)
        gh = jnp.where(
            lane_head[:, lo_lane : lo_lane + span] == one, 1.0, 0.0
        ).astype(BF16)
        for n, (i, j) in enumerate(pairs):
            ti = slice(i * GROUP, (i + 1) * GROUP)
            sj = slice(j * GROUP, (j + 1) * GROUP)
            gap = cum_col[ti] - cum_row[:, sj]
            if i == j:
                gap = jnp.where(causal, gap, -1e30)
            inner = mm(
                gs[ti, lo_lane : lo_lane + span] * gh, xs[sj, lo_lane : lo_lane + span], NT
            )
            mixed = jnp.exp(gap) * inner
            dscore[n] += mixed * rate_row[:, sj]
            q = score[n] * mixed
            c0 = jnp.sum(q, axis=0, keepdims=True)
            if i == j:
                gap = jnp.where(causal, gap, 0.0)
            c1 = jnp.sum(q * gap, axis=0, keepdims=True)
            c2 = jnp.sum(q * sig_col[ti], axis=0, keepdims=True)
            ra += rate_row[:, sj] * c1
            rb += rate_row[:, sj] * (c2 - sc_row[:, sj] * c0) + sig_row[:, sj] * c0
        ra_ref[at, :] = ra
        rb_ref[at, :] = rb

    @pl.when(k == pl.num_programs(0) - 1)
    def _():
        proj = proj_ref[...]
        b, c = proj[:, :half], proj[:, half:]
        dproj_ref[...] = jnp.zeros_like(dproj_ref)
        for n, (i, j) in enumerate(pairs):
            ti = slice(i * GROUP, (i + 1) * GROUP)
            sj = slice(j * GROUP, (j + 1) * GROUP)
            d = halves(dscore[n])
            dproj_ref[ti, half:] += mm3(d, halves(b[sj]))
            dproj_ref[sj, :half] += mm3(d, halves(c[ti]), TN)


def chain_kernel(count, decay_ref, fresh_ref, entry_ref, state_ref, back_ref,
                 got_f, got_b, out_f, out_b, send_f, recv_f, send_b, recv_b):
    me = lax.axis_index("seq")
    chunks = fresh_ref.shape[0]
    right = lax.rem(me + 1, count)
    left = lax.rem(me + count - 1, count)
    barrier = pltpu.get_barrier_semaphore()
    for peer in (left, right):
        pl.semaphore_signal(
            barrier, inc=1, device_id={"seq": peer}, device_id_type=pl.DeviceIdType.MESH
        )
    pl.semaphore_wait(barrier, 2)

    def forward(k):
        return pltpu.make_async_remote_copy(
            src_ref=out_f.at[k], dst_ref=got_f.at[k], send_sem=send_f.at[k],
            recv_sem=recv_f.at[k], device_id={"seq": right},
            device_id_type=pl.DeviceIdType.MESH,
        )

    def backward(k):
        return pltpu.make_async_remote_copy(
            src_ref=out_b.at[k], dst_ref=got_b.at[k], send_sem=send_b.at[k],
            recv_sem=recv_b.at[k], device_id={"seq": left},
            device_id_type=pl.DeviceIdType.MESH,
        )

    def skew(place):
        return 3 * (place // 2) + place % 2

    ahead = skew(me)
    behind = skew(count - 1 - me)

    def step(tau, unused):
        k = tau - ahead

        @pl.when((k >= 0) & (k < chunks))
        def _():
            @pl.when(me == 0)
            def _():
                state_ref[k] = jnp.zeros(state_ref.shape[1:], F32)
                out_f[k] = fresh_ref[k]

            @pl.when(me > 0)
            def _():
                forward(k).wait_recv()
                value = got_f[k]
                state_ref[k] = value
                out_f[k] = decay_ref[k] * value + fresh_ref[k]

            @pl.when(me < count - 1)
            def _():
                forward(k).start()

        j = tau - behind

        @pl.when((j >= 0) & (j < chunks))
        def _():
            @pl.when(me == count - 1)
            def _():
                back_ref[j] = jnp.zeros(back_ref.shape[1:], F32)
                out_b[j] = entry_ref[j]

            @pl.when(me < count - 1)
            def _():
                backward(j).wait_recv()
                value = got_b[j]
                back_ref[j] = value
                out_b[j] = decay_ref[j] * value + entry_ref[j]

            @pl.when(me > 0)
            def _():
                backward(j).start()

        return unused

    lax.fori_loop(0, chunks + 3 * ((count - 1) // 2) + (count - 1) % 2, step, 0)

    def drain(k, unused):
        @pl.when(me < count - 1)
        def _():
            forward(k).wait_send()

        @pl.when(me > 0)
        def _():
            backward(k).wait_send()

        return unused

    lax.fori_loop(0, chunks, drain, 0)


def back_kernel(
    width, x_ref, g_ref, state_ref, back_ref, proj_ref, cum_ref, rate_ref, sigcum_ref, sig_ref,
    dproj_ref, ra_ref, rb_ref, out_ref, heads_ref, whi, wlo, he, hf, gacc, acc,
):
    k = pl.program_id(0)
    length, heads = cum_ref.shape
    half = proj_ref.shape[1] // 2

    @pl.when(k == 0)
    def _():
        cum = cum_ref[...]
        for n, w in enumerate((jnp.exp(cum), jnp.exp(cum[length - 1 :] - cum) * rate_ref[...])):
            hi, lo = halves(w)
            whi[n] = hi
            wlo[n] = lo
        he[...] = jnp.zeros_like(he)
        hf[...] = jnp.zeros_like(hf)
        gacc[...] = jnp.zeros_like(gacc)
        acc[...] = dproj_ref[...]

    lanes = x_ref.shape[1]
    first = k * (lanes // width)
    hot = spread(heads, lanes, width, first)
    cold = gathers(heads, lanes, width, first)
    xf = x_ref[...].astype(F32)
    gf = g_ref[...].astype(F32)
    state = state_ref[0]
    back = back_ref[0]
    state2 = halves(state)
    back2 = halves(back)
    proj = proj_ref[...]
    grow = mm(whi[0], hot) + mm(wlo[0], hot)
    fade = mm(whi[1], hot) + mm(wlo[1], hot)
    hi, lo = halves(gf * mm3(halves(proj[:, half:]), state2))
    he[...] += mm(hi, cold) + mm(lo, cold)
    hi, lo = halves(xf * mm3(halves(proj[:, :half]), back2))
    hf[...] += mm(hi, cold) + mm(lo, cold)
    acc[:, half:] += mm3(halves(grow * gf), state2, NT)
    acc[:, :half] += mm3(halves(fade * xf), back2, NT)
    both = jnp.broadcast_to(jnp.sum(state * back, axis=0, keepdims=True), (8, lanes))
    hi, lo = halves(both)
    gacc[...] += mm(hi, cold) + mm(lo, cold)

    @pl.when(k == pl.num_programs(0) - 1)
    def _():
        cum = cum_ref[...]
        sigcum = sigcum_ref[...]
        last = cum[length - 1 :]
        sig_last = sigcum[length - 1 :]
        e = jnp.exp(cum) * he[...]
        f0 = jnp.exp(last - cum) * hf[...]
        f = f0 * rate_ref[...]
        link = jnp.exp(last) * gacc[0:1, :]
        ga = jnp.sum(e * cum + f * (last - cum), axis=0, keepdims=True) + link * last
        gb = (
            jnp.sum(e * sigcum + f * (sig_last - sigcum) + f0 * sig_ref[...], axis=0, keepdims=True)
            + link * sig_last
        )
        heads_ref[0:1, :] = ga + jnp.sum(ra_ref[...].T, axis=0, keepdims=True)
        heads_ref[1:2, :] = gb + jnp.sum(rb_ref[...].T, axis=0, keepdims=True)
        out_ref[...] = acc[...].astype(BF16)


def local(
    count, tokens, values, out_grad, w_bc, w_dt, a_log, dt_bias, fire_flags,
    last_bc, last_heads, total_bc, total_heads,
):
    tok = tokens[0]
    x = values[0]
    g = out_grad[0]
    length, inner = x.shape
    heads = a_log.shape[0]
    width = inner // heads
    chunks = inner // LANES
    wide = w_bc.shape[1]
    half = wide // 2
    blocks = length // GROUP
    npairs = blocks * (blocks + 1) // 2
    sds = jax.ShapeDtypeStruct
    whole = lambda a: pl.BlockSpec(a.shape, lambda k: (0,) * len(a.shape))
    chunk2 = pl.BlockSpec((length, LANES), lambda k: (0, k))
    chunk3 = pl.BlockSpec((1, half, LANES), lambda k: (k, 0, 0))
    small = sds((length, heads), F32)
    states = sds((chunks, half, LANES), F32)
    outs = [states, states, sds((length, wide), F32), small, small, small, small,
            sds((length, wide), F32), sds((heads, GROUP), F32), sds((heads, GROUP), F32)]
    alog2 = a_log[None]
    bias2 = dt_bias[None]
    fresh, entry, proj, cum, rate, sigcum, sig, dproj, ra, rb = pl.pallas_call(
        functools.partial(front_kernel, width),
        grid=(chunks,),
        in_specs=[whole(tok), whole(w_bc), whole(w_dt), whole(alog2), whole(bias2), chunk2, chunk2],
        out_specs=[chunk3, chunk3] + [whole(o) for o in outs[2:]],
        out_shape=outs,
        scratch_shapes=[
            pltpu.VMEM((2, length, heads), BF16),
            pltpu.VMEM((2, length, heads), BF16),
            pltpu.VMEM((5, length, heads), BF16),
            pltpu.VMEM((4, heads, length), F32),
            pltpu.VMEM((npairs, GROUP, GROUP), F32),
            pltpu.VMEM((npairs, GROUP, GROUP), F32),
        ],
        name="front",
    )(tok, w_bc, w_dt, alog2, bias2, x, g)
    decay = jnp.repeat(jnp.exp(cum[length - 1]), width).reshape(chunks, 1, LANES)
    vm = pl.BlockSpec(memory_space=pltpu.VMEM)
    buf = pltpu.VMEM((chunks, half, LANES), F32)
    sem = pltpu.SemaphoreType.DMA((chunks,))
    state, back = pl.pallas_call(
        functools.partial(chain_kernel, count),
        in_specs=[vm, vm, vm],
        out_specs=[vm, vm],
        out_shape=[states, states],
        scratch_shapes=[buf, buf, buf, buf, sem, sem, sem, sem],
        compiler_params=pltpu.CompilerParams(
            collective_id=0, has_side_effects=True, vmem_limit_bytes=56 * 1024 * 1024
        ),
        name="chain",
    )(decay, fresh, entry)
    d_projected, grad_heads = pl.pallas_call(
        functools.partial(back_kernel, width),
        grid=(chunks,),
        in_specs=[chunk2, chunk2, chunk3, chunk3]
        + [whole(a) for a in (proj, cum, rate, sigcum, sig, dproj, ra, rb)],
        out_specs=[whole(proj), pl.BlockSpec((2, heads), lambda k: (0, 0))],
        out_shape=[sds((length, wide), BF16), sds((2, heads), F32)],
        scratch_shapes=[
            pltpu.VMEM((2, length, heads), BF16),
            pltpu.VMEM((2, length, heads), BF16),
            pltpu.VMEM((length, heads), F32),
            pltpu.VMEM((length, heads), F32),
            pltpu.VMEM((8, heads), F32),
            pltpu.VMEM((length, wide), F32),
        ],
        name="back",
    )(x, g, state, back, proj, cum, rate, sigcum, sig, dproj, ra, rb)
    grad_bc = mm(tok, d_projected, TN)
    own_last = last_bc[0]
    own_rows = lax.psum_scatter(grad_bc, "seq", scatter_dimension=0, tiled=True)
    diff_bc = own_rows - own_last
    square_bc, summed_heads = lax.psum((jnp.sum(diff_bc * diff_bc), grad_heads), "seq")
    diff_heads = summed_heads - last_heads[0]
    trigger = jnp.sqrt(square_bc + jnp.sum(diff_heads * diff_heads) + 1e-06)
    weight = fire_flags[0].astype(F32)
    fired_bc, fired_heads = lax.psum((weight * diff_bc, weight * diff_heads), "dp")
    new_total_bc = total_bc + fired_bc
    new_total_heads = total_heads + fired_heads
    new_last_bc = jnp.where(fire_flags[0] > 0, own_rows, own_last)[None]
    new_last_heads = jnp.where(fire_flags[0] > 0, summed_heads, last_heads[0])[None]
    return (new_total_bc, new_total_heads, new_last_bc, new_last_heads, trigger.reshape(1))


def solution(mesh):
    in_specs = (
        P("dp", "seq", None), P("dp", "seq", None), P("dp", "seq", None), P(), P(), P(), P(),
        P("dp"), P("dp", "seq", None), P("dp", None, None), P("seq", None), P(),
    )
    out_specs = (P("seq", None), P(), P("dp", "seq", None), P("dp", None, None), P("dp"))
    return jax.shard_map(
        functools.partial(local, mesh.shape["seq"]), mesh=mesh, in_specs=in_specs,
        out_specs=out_specs, check_vma=False,
    )
```

time: 917 us -> 223 us (0.24)
  waiting for transfers between devices: 472 us -> 49.2 us
  matrix products: 136 us -> 1.92 us
  local copies, waits for them, and re-layouts: 132 us -> 9.15 us
  Pallas kernels: 0 us -> 115 us
  other arithmetic: 85.7 us -> 4.18 us
  loops' own time: 26.4 us -> 0 us
  blocking collectives: 39.6 us -> 25.8 us
    all_gather x2 -> x0, waiting for transfers between devices: 323 us -> none  [prefix(): gathered = jax.tree.map(lambda a: lax.all_gather(a, axis), part)]
    dot_general x27 -> x1, matrix products: 136 us -> 1.92 us  [mm(): return lax.dot_general(a, b, dims, preferred_element_type=F32)]
    pallas_call x0 -> x3, Pallas kernels: none -> 115 us  [the longest x1 55.6 us: local(): pl.pallas_call(functools.partial(chain_kernel, count), in_specs=[vm, vm,...]
    unnamed x5 -> x3, waiting for transfers between devices: 136 us -> 35.3 us
    dynamic_slice x24 -> x0, local copies, waits for them, and re-layouts: 67.6 us -> none  [the longest x14 61.5 us: one(): lax.dynamic_index_in_dim(a, source, 0, False)]
    add x7 -> x0, other arithmetic: 48.2 us -> none  [combine_states(): later[0][:, None, None] * earlier[1] + later[1]]
    another operation x4 -> x0, loops' own time: 26.4 us -> none  [the longest x2 25.9 us: sequence_loss(): lax.scan(jax.checkpoint(group_terms), (state_start, jnp.zeros((), jnp.flo...]
    all_gather x1 -> x0, blocking collectives: 14.1 us -> none  [prefix(): gathered = jax.tree.map(lambda a: lax.all_gather(a, axis), part)]
  transfers between devices with their start and end apart: 4 -> 2, of which waited for: 4 -> 2; matrix products, arithmetic and copies ran while one was open for 5% -> 1% of each run, Pallas kernels for 0% -> 0%
where the time goes in v1:
time: 223 us
  Pallas kernels  115 us (52%)
  waiting for transfers between devices  49.2 us (22%)
  blocking collectives  25.8 us (12%)
  between operations  17.3 us (8%)
  local copies, waits for them, and re-layouts  9.15 us (4%)
  other arithmetic  4.18 us (2%)
    pallas_call x1, Pallas kernels, local(): pl.pallas_call(functools.partial(chain_kernel, count), in_specs=[vm, vm,...  55.6 us
    unnamed x3, waiting for transfers between devices  35.3 us
    pallas_call x1, Pallas kernels, local(): pl.pallas_call(functools.partial(front_kernel, width), grid=(chunks,), in...  30.4 us
    pallas_call x1, Pallas kernels, local(): pl.pallas_call(functools.partial(back_kernel, width), grid=(chunks,), in_...  29 us
    psum x1, blocking collectives, local(): lax.psum((jnp.sum(diff_bc * diff_bc), grad_heads), 'seq')  15.8 us
    psum x1, waiting for transfers between devices, local(): lax.psum((weight * diff_bc, weight * diff_heads), 'dp')  13.9 us
    psum x1, blocking collectives, local(): lax.psum((weight * diff_bc, weight * diff_heads), 'dp')  10 us
    unnamed x17, local copies, waits for them, and re-layouts  7.59 us
  transfers between devices with their start and end apart: 2, of which 2 were waited for; matrix products, arithmetic and copies ran while one was open for 1% of the time, Pallas kernels for 0%

profile of v1, /device:TPU:0, one launch (start us, length us, event | category | flops | bytes accessed | tf_op | source)
XLA Modules:
  0.0 222.7 jit_solution(8847928228032265185)
XLA Ops:
  7.2 0.0 reduce-scatter.4.cloned.1.call-start
  7.2 2.1 copy.27.wdt_ref
  9.3 30.4 %front.1 = (f32[20,128,256]{2,1,0:T(8,128)}, f32[20,128,256]{2,1,0:T(8,128)}, f32[256,256]{1,0:T(8,128)}, f32[256,80]{1,0:T(8,128)}, f32[256,80]{1,0:T(8,128)}, ...) custom-call(bf16[256,2560]{1,0:T(8,128)(2,1)} %bitcast.40, ...), custom_call_target="tpu_custom_call" | custom-call | tf_op jit(solution)/shard_map/front/pallas_call | solution.py:344
  39.7 0.7 exponential_reduce_fusion
  40.4 0.1 exp.8
  40.5 0.1 broadcast_in_dim.19
  40.6 0.7 broadcast_in_dim.20.decay_ref
  41.3 55.6 %chain.1 = (f32[20,128,256]{2,1,0:T(8,128)}, f32[20,128,256]{2,1,0:T(8,128)}) custom-call(f32[20,1,256]{2,1,0:T(1,128)} %broadcast_in_dim.20.decay_ref, f32[20,128,256]{2,1,0:T(8,128)} %get-tuple-element.20.fresh_ref, f32[20,128,256]{2,1,0:T(8,128)} %get-tuple-element.21.entry_ref), custom_call_target="tpu_custom_call" | custom-call | tf_op jit(solution)/shard_map/chain/pallas_call | solution.py:364
  97.0 29.0 %back.1 = (bf16[256,256]{1,0:T(8,128)(2,1)}, f32[2,80]{1,0:T(2,128)}) custom-call(bf16[256,5120]{1,0:T(8,128)(2,1)} %bitcast.37, bf16[256,5120]{1,0:T(8,128)(2,1)} %bitcast.39, f32[20,128,256]{2,1,0:T(8,128)} %get-tuple-element.22.state_ref, f32[20,128,256]{2,1,0:T(8,128)} %get-tuple-element.23.back_ref, f32[256,256]{1,0:T(8,128)} %get-tuple-element.24.proj_ref, ...), custom_call_target="tpu_custom_call" | custom-call | tf_op jit(solution)/shard_map/back/pallas_call | solution.py:375
  126.0 1.9 convolution_bitcast_fusion
  127.9 2.1 copy.32
  130.0 0.0 copy-start
  130.0 0.0 copy-start.1
  130.0 0.0 reduce-scatter.4.cloned.1.call-update
  130.0 0.0 copy-start.4
  130.1 0.0 copy-start.3
  130.1 0.0 copy-start.2
  130.1 0.0 all-reduce.3.cloned.1.call-start
  130.8 0.2 copy-done
  131.0 0.2 copy.28
  131.2 35.3 %reduce-scatter.4.cloned.1.call-done = f32[320,256]{1,0:T(8,128)} async-done(((f32[2560,256]{1,0:T(8,128)}), f32[320,256]{1,0:T(8,128)}) %reduce-scatter.4.cloned.1.call-update) | async-done | bytes 327696
  166.5 1.1 copy.33
  167.6 1.4 fusion
  169.0 0.0 all-reduce.3.cloned.1.call-update
  169.0 0.0 copy-done.1
  169.0 0.2 copy.29
  169.2 0.0 copy-done.4
  169.2 15.8 %all-reduce = (f32[2,80]{1,0:T(2,128)S(1)}, f32[]{:T(128)}) all-reduce(f32[2,80]{1,0:T(2,128)S(1)} %copy-done.4, f32[]{:T(128)} %get-tuple-element.51), channel_id=1, replica_groups=mesh['dp'=4,'seq'=8] {'seq'}, use_global_device_ids=true, to_apply=%region_2.0 | all-reduce | flops 161 | bytes 1288 | tf_op jit(solution)/shard_map/psum | solution.py:396
  185.0 0.0 copy-done.3
  185.0 1.2 multiply_reduce_fusion.1
  187.5 0.9 copy.31
  188.4 10.0 %psum.30 = f32[2,80]{1,0:T(2,128)S(1)} all-reduce(f32[2,80]{1,0:T(2,128)S(1)} %get-tuple-element.55), channel_id=1, replica_groups=mesh['dp'=4,'seq'=8] {'dp'}, use_global_device_ids=true, to_apply=%region_3.0 | all-reduce | flops 160 | bytes 1280 | tf_op jit(solution)/shard_map/psum | solution.py:400
  198.4 0.0 copy-done.2
  198.4 0.6 add.23
  199.0 13.9 %all-reduce.3.cloned.1.call-done = f32[320,256]{0,1:T(8,128)} async-done(((f32[320,256]{0,1:T(8,128)}), f32[320,256]{0,1:T(8,128)}) %all-reduce.3.cloned.1.call-update) | async-done | bytes 327696 | tf_op jit(solution)/shard_map/psum | solution.py:400
  212.9 1.0 add.22
  213.9 0.9 copy.30
Async XLA Ops:
  7.2 159.3 %reduce-scatter.4.cloned.1.call-start = ((), (), s32[]{:S(2)}) async-start(), calls=%async_computation.2 | async-start | bytes 2949120
  130.0 1.0 copy-start
  130.0 39.0 %copy-start.1 = (f32[320,256]{1,0:T(8,128)S(1)}, f32[320,256]{1,0:T(8,128)}, u32[]{:S(2)}) copy-start(f32[320,256]{1,0:T(8,128)} %param.22) | copy-start | bytes 983044
  130.0 39.2 %copy-start.4 = (f32[2,80]{1,0:T(2,128)S(1)}, f32[2,80]{1,0:T(2,128)}, u32[]{:S(2)}) copy-start(f32[2,80]{1,0:T(2,128)} %get-tuple-element.32) | copy-start | bytes 1924
  130.1 54.9 %copy-start.3 = (f32[1,2,80]{2,1,0:T(2,128)S(1)}, f32[1,2,80]{2,1,0:T(2,128)}, u32[]{:S(2)}) copy-start(f32[1,2,80]{2,1,0:T(2,128)} %param.21) | copy-start | bytes 1924
  130.1 68.3 %copy-start.2 = (f32[2,80]{1,0:T(2,128)S(1)}, f32[2,80]{1,0:T(2,128)}, u32[]{:S(2)}) copy-start(f32[2,80]{1,0:T(2,128)} %param.23) | copy-start | bytes 1924
  130.1 82.8 %all-reduce.3.cloned.1.call-start = ((), (), s32[]{:S(2)}) async-start(), calls=%async_computation.1 | async-start | bytes 786432 | tf_op jit(solution)/shard_map/psum | solution.py:400
Sparse Core Ops, SparseCore 0:
  130.2 36.2 reduce-scatter.3
  169.4 43.3 all-reduce.2

commit v2 on v1

--- a/solution.py
+++ b/solution.py
@@ -62,7 +62,7 @@
         tok = tok_ref[...]
         proj = mm(tok, wbc_ref[...])
         proj_ref[...] = proj
-        z = mm(tok, wdt_ref[...]) + bias_ref[...]
+        z = mm(tok, wdt_ref[...], NT) + bias_ref[...]
         tail = jnp.exp(-jnp.abs(z))
         rate = jnp.maximum(z, 0.0) + jnp.log1p(tail)
         sig = jnp.where(z >= 0, 1.0, tail) / (1.0 + tail)
@@ -188,9 +188,6 @@
             device_id_type=pl.DeviceIdType.MESH,
         )
 
-    def skew(place):
-        return 3 * (place // 2) + place % 2
-
     ahead = skew(me)
     behind = skew(count - 1 - me)
 
@@ -316,8 +313,173 @@
         out_ref[...] = acc[...].astype(BF16)
 
 
+def remote(src, dst, send, recv, axis, peer):
+    return pltpu.make_async_remote_copy(
+        src_ref=src, dst_ref=dst, send_sem=send, recv_sem=recv, device_id={axis: peer},
+        device_id_type=pl.DeviceIdType.MESH,
+    )
+
+
+def skew(place):
+    return 3 * (place // 2) + place % 2
+
+
+def tail_kernel(
+    count, replicas, tok_ref, dproj_ref, heads_ref, last_ref, last_heads_ref, weight_ref,
+    rows_ref, fired_ref, sum_ref, fired_heads_ref, square_ref,
+    own, got_r, got_l, pay, dgot, hgot, hmine, sgot, smine,
+    send_r, recv_r, send_l, recv_l, send_d, recv_d, send_h, recv_h, send_s, recv_s,
+):
+    me = lax.axis_index("seq")
+    mine = lax.axis_index("dp")
+    rows = last_ref.shape[0]
+    half = rows // 2
+    wide = last_ref.shape[1]
+    stages = replicas.bit_length() - 1
+
+    def partner(bit):
+        size = 2**bit
+        return mine + size * (1 - 2 * (mine // size % 2))
+
+    barrier = pltpu.get_barrier_semaphore()
+    for d in range(1, count):
+        pl.semaphore_signal(
+            barrier, inc=1, device_id={"seq": lax.rem(me + d, count)},
+            device_id_type=pl.DeviceIdType.MESH,
+        )
+    for bit in range(stages):
+        pl.semaphore_signal(
+            barrier, inc=1, device_id={"dp": partner(bit)}, device_id_type=pl.DeviceIdType.MESH
+        )
+
+    hmine[...] = heads_ref[...]
+    hgot[me] = heads_ref[...]
+    tok_rows = tok_ref.shape[1] // wide
+    dproj = dproj_ref[...]
+    for n in range(tok_rows):
+        own[n * wide : (n + 1) * wide, :] = mm(tok_ref[:, n * wide : (n + 1) * wide], dproj, TN)
+    pl.semaphore_wait(barrier, count - 1 + stages)
+
+    def to_peer(d, src, got, send, recv):
+        return remote(
+            src, got.at[me], send.at[d], recv.at[me], "seq", lax.rem(me + d, count)
+        )
+
+    def from_peer(d, src, got, send, recv):
+        place = lax.rem(me + d, count)
+        return remote(src, got.at[place], send.at[d], recv.at[place], "seq", place)
+
+    def block(j):
+        return own.at[pl.ds(pl.multiple_of(j * rows, 8), rows)]
+
+    def step(tau, unused):
+        t = tau - skew(me)
+        j = count - 1 - t
+
+        @pl.when((t >= 0) & (j >= me))
+        def _():
+            ref = block(j)
+
+            @pl.when(me > 0)
+            def _():
+                remote(ref, got_r.at[j], send_r.at[j], recv_r.at[j], "seq", me - 1).wait_recv()
+                ref[...] += got_r[j]
+
+            @pl.when(j > me)
+            def _():
+                remote(ref, got_r.at[j], send_r.at[j], recv_r.at[j], "seq", me + 1).start()
+
+        u = tau - skew(count - 1 - me)
+
+        @pl.when((u >= 0) & (u <= me))
+        def _():
+            ref = block(u)
+
+            @pl.when(me < count - 1)
+            def _():
+                remote(ref, got_l.at[u], send_l.at[u], recv_l.at[u], "seq", me + 1).wait_recv()
+                ref[...] += got_l[u]
+
+            @pl.when(u < me)
+            def _():
+                remote(ref, got_l.at[u], send_l.at[u], recv_l.at[u], "seq", me - 1).start()
+
+        return unused
+
+    for d in range(1, count):
+        to_peer(d, hmine, hgot, send_h, recv_h).start()
+    lax.fori_loop(0, count + skew(count - 1), step, 0)
+
+    for d in range(1, count):
+        from_peer(d, hmine, hgot, send_h, recv_h).wait_recv()
+    summed = hgot[0]
+    for n in range(1, count):
+        summed = summed + hgot[n]
+    sum_ref[...] = summed
+    own_rows = block(me)[...]
+    rows_ref[...] = own_rows
+    diff = own_rows - last_ref[...]
+    square = jnp.sum(diff * diff, axis=0, keepdims=True)
+    square = sum(square[:, n * GROUP : (n + 1) * GROUP] for n in range(wide // GROUP))
+    square = jnp.broadcast_to(square, smine.shape)
+    weight = weight_ref[0:1, :]
+    weighted = diff * weight
+    for h in range(2):
+        pay[h, 0, :half, :] = weighted[h * half : (h + 1) * half]
+        pay[h, 0, half:, :] = jnp.zeros((8, wide), F32)
+    pay[0, 0, half:, :GROUP] = (summed - last_heads_ref[...]) * weight[:, :GROUP]
+
+    def swap(h, s):
+        bit = s if h == 0 else stages - 1 - s
+        return remote(
+            pay.at[h, s], dgot.at[h, s], send_d.at[h, s], recv_d.at[h, s], "dp", partner(bit)
+        )
+
+    for h in range(2):
+        swap(h, 0).start()
+    smine[...] = square
+    sgot[me] = square
+    for d in range(1, count):
+        to_peer(d, smine, sgot, send_s, recv_s).start()
+    for s in range(stages):
+        for h in range(2):
+            swap(h, s).wait_recv()
+            pay[h, s + 1] = pay[h, s] + dgot[h, s]
+            if s + 1 < stages:
+                swap(h, s + 1).start()
+    for h in range(2):
+        fired_ref[h * half : (h + 1) * half, :] = pay[h, stages, :half, :]
+    fired_heads_ref[...] = pay[0, stages, half:, :GROUP]
+    for d in range(1, count):
+        from_peer(d, smine, sgot, send_s, recv_s).wait_recv()
+    total = sgot[0]
+    for n in range(1, count):
+        total = total + sgot[n]
+    square_ref[...] = total
+
+    for s in range(stages):
+        for h in range(2):
+            swap(h, s).wait_send()
+    for d in range(1, count):
+        to_peer(d, hmine, hgot, send_h, recv_h).wait_send()
+        to_peer(d, smine, sgot, send_s, recv_s).wait_send()
+
+    def drain(j, unused):
+        @pl.when(j > me)
+        def _():
+            remote(block(j), got_r.at[j], send_r.at[j], recv_r.at[j], "seq", me + 1).wait_send()
+
+        @pl.when(j < me)
+        def _():
+            remote(block(j), got_l.at[j], send_l.at[j], recv_l.at[j], "seq", me - 1).wait_send()
+
+        return unused
+
+    lax.fori_loop(0, count, drain, 0)
+
+
 def local(
-    count, tokens, values, out_grad, w_bc, w_dt, a_log, dt_bias, fire_flags,
+    count, replicas, tokens, values, out_grad, w_bc, w_dt, a_log, dt_bias, fire_flags,
     last_bc, last_heads, total_bc, total_heads,
 ):
     tok = tokens[0]
@@ -341,10 +503,11 @@
             sds((length, wide), F32), sds((heads, GROUP), F32), sds((heads, GROUP), F32)]
     alog2 = a_log[None]
     bias2 = dt_bias[None]
+    wdt = w_dt.T
     fresh, entry, proj, cum, rate, sigcum, sig, dproj, ra, rb = pl.pallas_call(
         functools.partial(front_kernel, width),
         grid=(chunks,),
-        in_specs=[whole(tok), whole(w_bc), whole(w_dt), whole(alog2), whole(bias2), chunk2, chunk2],
+        in_specs=[whole(tok), whole(w_bc), whole(wdt), whole(alog2), whole(bias2), chunk2, chunk2],
         out_specs=[chunk3, chunk3] + [whole(o) for o in outs[2:]],
         out_shape=outs,
         scratch_shapes=[
@@ -356,7 +519,7 @@
             pltpu.VMEM((npairs, GROUP, GROUP), F32),
         ],
         name="front",
-    )(tok, w_bc, w_dt, alog2, bias2, x, g)
+    )(tok, w_bc, wdt, alog2, bias2, x, g)
     decay = jnp.repeat(jnp.exp(cum[length - 1]), width).reshape(chunks, 1, LANES)
     vm = pl.BlockSpec(memory_space=pltpu.VMEM)
     buf = pltpu.VMEM((chunks, half, LANES), F32)
@@ -389,17 +552,39 @@
         ],
         name="back",
     )(x, g, state, back, proj, cum, rate, sigcum, sig, dproj, ra, rb)
-    grad_bc = mm(tok, d_projected, TN)
     own_last = last_bc[0]
-    own_rows = lax.psum_scatter(grad_bc, "seq", scatter_dimension=0, tiled=True)
-    diff_bc = own_rows - own_last
-    square_bc, summed_heads = lax.psum((jnp.sum(diff_bc * diff_bc), grad_heads), "seq")
+    rows = own_last.shape[0]
+    stages = replicas.bit_length() - 1
+    tile = lambda a: jnp.pad(a, ((0, 8 - a.shape[0]), (0, GROUP - a.shape[1])))
+    weight = jnp.broadcast_to(fire_flags[0].astype(F32), (8, wide))
+    dma = pltpu.SemaphoreType.DMA
+    own_rows, fired_bc, summed, fired, square = pl.pallas_call(
+        functools.partial(tail_kernel, count, replicas),
+        in_specs=[vm] * 6,
+        out_specs=[vm] * 5,
+        out_shape=[sds((rows, wide), F32)] * 2 + [sds((8, GROUP), F32)] * 3,
+        scratch_shapes=[
+            pltpu.VMEM((rows * count, wide), F32),
+            pltpu.VMEM((count, rows, wide), F32),
+            pltpu.VMEM((count, rows, wide), F32),
+            pltpu.VMEM((2, stages + 1, rows // 2 + 8, wide), F32),
+            pltpu.VMEM((2, stages, rows // 2 + 8, wide), F32),
+            pltpu.VMEM((count, 8, GROUP), F32),
+            pltpu.VMEM((8, GROUP), F32),
+            pltpu.VMEM((count, 8, GROUP), F32),
+            pltpu.VMEM((8, GROUP), F32),
+        ]
+        + [dma((count,))] * 4 + [dma((2, stages))] * 2 + [dma((count,))] * 4,
+        compiler_params=pltpu.CompilerParams(
+            collective_id=1, has_side_effects=True, vmem_limit_bytes=48 * 1024 * 1024
+        ),
+        name="tail",
+    )(tok, d_projected, tile(grad_heads), own_last, tile(last_heads[0]), weight)
+    summed_heads = summed[:2, :heads]
     diff_heads = summed_heads - last_heads[0]
-    trigger = jnp.sqrt(square_bc + jnp.sum(diff_heads * diff_heads) + 1e-06)
-    weight = fire_flags[0].astype(F32)
-    fired_bc, fired_heads = lax.psum((weight * diff_bc, weight * diff_heads), "dp")
+    trigger = jnp.sqrt(jnp.sum(square[0]) + jnp.sum(diff_heads * diff_heads) + 1e-06)
     new_total_bc = total_bc + fired_bc
-    new_total_heads = total_heads + fired_heads
+    new_total_heads = total_heads + fired[:2, :heads]
     new_last_bc = jnp.where(fire_flags[0] > 0, own_rows, own_last)[None]
     new_last_heads = jnp.where(fire_flags[0] > 0, summed_heads, last_heads[0])[None]
     return (new_total_bc, new_total_heads, new_last_bc, new_last_heads, trigger.reshape(1))
@@ -412,6 +597,6 @@
     )
     out_specs = (P("seq", None), P(), P("dp", "seq", None), P("dp", None, None), P("dp"))
     return jax.shard_map(
-        functools.partial(local, mesh.shape["seq"]), mesh=mesh, in_specs=in_specs,
+        functools.partial(local, mesh.shape["seq"], mesh.shape["dp"]), mesh=mesh, in_specs=in_specs,
         out_specs=out_specs, check_vma=False,
     )

time: 223 us -> 167 us (0.75)
  waiting for transfers between devices: 49.2 us -> 0 us
  Pallas kernels: 115 us -> 156 us
  blocking collectives: 25.8 us -> 0 us
  between operations: 17.3 us -> 3.9 us
  local copies, waits for them, and re-layouts: 9.15 us -> 3.18 us
    pallas_call x0 -> x1, Pallas kernels: none -> 40.7 us  [local(): pl.pallas_call(functools.partial(tail_kernel, count, replicas), in_specs=...]
    unnamed x3 -> x0, waiting for transfers between devices: 35.3 us -> none
    psum x2 -> x0, blocking collectives: 25.8 us -> none  [the longest x1 15.8 us: local(): lax.psum((jnp.sum(diff_bc * diff_bc), grad_heads), 'seq')]
    psum x1 -> x0, waiting for transfers between devices: 13.9 us -> none  [local(): lax.psum((weight * diff_bc, weight * diff_heads), 'dp')]
    unnamed x17 -> x12, local copies, waits for them, and re-layouts: 7.59 us -> 0.93 us
  transfers between devices with their start and end apart: 2 -> 0, of which waited for: 2 -> 0; matrix products, arithmetic and copies ran while one was open for 1% -> 0% of each run, Pallas kernels for 0% -> 0%
where the time goes in v2:
time: 167 us; the launch traced here: 166 us
  Pallas kernels  156 us (93%)
  between operations  3.9 us (2%)
  other arithmetic  3.3 us (2%)
  local copies, waits for them, and re-layouts  3.18 us (2%)
    pallas_call x1, Pallas kernels, local(): pl.pallas_call(functools.partial(chain_kernel, count), in_specs=[vm, vm,...  55.6 us
    pallas_call x1, Pallas kernels, local(): pl.pallas_call(functools.partial(tail_kernel, count, replicas), in_specs=...  40.7 us
    pallas_call x1, Pallas kernels, local(): pl.pallas_call(functools.partial(front_kernel, width), grid=(chunks,), in...  30.3 us
    pallas_call x1, Pallas kernels, local(): pl.pallas_call(functools.partial(back_kernel, width), grid=(chunks,), in_...  29.1 us

profile of v2, /device:TPU:0, one launch (start us, length us, event | category | flops | bytes accessed | tf_op | source)
XLA Modules:
  0.0 166.2 jit_solution(12945901924871610240)
XLA Ops:
  0.6 30.3 %front.1 = (f32[20,128,256]{2,1,0:T(8,128)}, f32[20,128,256]{2,1,0:T(8,128)}, f32[256,256]{1,0:T(8,128)}, f32[256,80]{1,0:T(8,128)}, f32[256,80]{1,0:T(8,128)}, ...) custom-call(bf16[256,2560]{1,0:T(8,128)(2,1)} %bitcast.18, ...), custom_call_target="tpu_custom_call" | custom-call | tf_op jit(solution)/shard_map/front/pallas_call | solution.py:507
  31.0 0.7 exponential_reduce_fusion
  31.7 0.1 exp.8
  31.7 0.1 broadcast_in_dim.22
  31.8 0.7 broadcast_in_dim.23.decay_ref
  32.5 55.6 %chain.1 = (f32[20,128,256]{2,1,0:T(8,128)}, f32[20,128,256]{2,1,0:T(8,128)}) custom-call(f32[20,1,256]{2,1,0:T(1,128)} %broadcast_in_dim.23.decay_ref, f32[20,128,256]{2,1,0:T(8,128)} %get-tuple-element.25.fresh_ref, f32[20,128,256]{2,1,0:T(8,128)} %get-tuple-element.26.entry_ref), custom_call_target="tpu_custom_call" | custom-call | tf_op jit(solution)/shard_map/chain/pallas_call | solution.py:527
  88.2 0.0 copy-start.4
  88.2 0.0 copy-start
  88.2 0.0 copy-start.1
  88.2 0.0 copy-start.5
  88.2 0.0 copy-start.3
  88.2 29.1 %back.1 = (bf16[256,256]{1,0:T(8,128)(2,1)}, f32[2,80]{1,0:T(2,128)}) custom-call(bf16[256,5120]{1,0:T(8,128)(2,1)} %bitcast.22, bf16[256,5120]{1,0:T(8,128)(2,1)} %bitcast.24, f32[20,128,256]{2,1,0:T(8,128)} %get-tuple-element.27.state_ref, f32[20,128,256]{2,1,0:T(8,128)} %get-tuple-element.28.back_ref, f32[256,256]{1,0:T(8,128)} %get-tuple-element.29.proj_ref, ...), custom_call_target="tpu_custom_call" | custom-call | tf_op jit(solution)/shard_map/back/pallas_call | solution.py:538
  117.4 0.7 pad.7.heads_ref
  118.7 0.0 copy-done.4
  118.7 0.0 copy-done
  118.7 0.0 copy-done.1
  118.7 0.0 copy-start.2
  118.8 0.9 copy-done.2
  119.7 40.7 %tail.1 = (f32[320,256]{1,0:T(8,128)S(1)}, f32[320,256]{1,0:T(8,128)S(1)}, f32[8,128]{1,0:T(8,128)S(1)}, f32[8,128]{1,0:T(8,128)S(1)}, f32[8,128]{1,0:T(8,128)S(1)}) custom-call(bf16[256,2560]{1,0:T(8,128)(2,1)S(1)} %bitcast.19, bf16[256,256]{1,0:T(8,128)(2,1)S(1)} %copy-done.2, f32[8,128]{1,0:T(8,128)S(1)} %pad.7.heads_ref, f32[320,256]{1,0:T(8,128)S(1)} %bitcast.20, ...), custom_call_target="tpu_custom_call" | custom-call | tf_op jit(solution)/shard_map/tail/pallas_call | solution.py:561
  160.4 0.0 copy-done.5
  160.4 1.2 multiply_reduce_fusion
  161.6 0.6 slice_reduce_fusion
  163.5 0.8 select_bitcast_fusion
  164.3 0.0 copy-done.3
  164.3 0.8 add.16
  (2 shorter events, 0.0 us)
Async XLA Ops:
  88.2 30.6 %copy-start.4 = (f32[1,2,80]{2,1,0:T(2,128)S(1)}, f32[1,2,80]{2,1,0:T(2,128)}, u32[]{:S(2)}) copy-start(f32[1,2,80]{2,1,0:T(2,128)} %param.21) | copy-start | bytes 1924
  88.2 30.6 %copy-start = (bf16[1,256,2560]{2,1,0:T(8,128)(2,1)S(1)}, bf16[1,256,2560]{2,1,0:T(8,128)(2,1)}, u32[]{:S(2)}) copy-start(bf16[1,256,2560]{2,1,0:T(8,128)(2,1)} %param.12) | copy-start | bytes 3932164
  88.2 30.6 %copy-start.1 = (f32[1,320,256]{2,1,0:T(8,128)S(1)}, f32[1,320,256]{2,1,0:T(8,128)}, u32[]{:S(2)}) copy-start(f32[1,320,256]{2,1,0:T(8,128)} %param.20) | copy-start | bytes 983044
  88.2 72.2 %copy-start.5 = (f32[2,80]{1,0:T(2,128)S(1)}, f32[2,80]{1,0:T(2,128)}, u32[]{:S(2)}) copy-start(f32[2,80]{1,0:T(2,128)} %param.23) | copy-start | bytes 1924
  88.2 76.1 %copy-start.3 = (f32[320,256]{1,0:T(8,128)S(1)}, f32[320,256]{1,0:T(8,128)}, u32[]{:S(2)}) copy-start(f32[320,256]{1,0:T(8,128)} %param.22) | copy-start | bytes 983044
  118.7 0.9 copy-start.2

commit v3 on v2

--- a/solution.py
+++ b/solution.py
@@ -48,20 +48,16 @@
 
 def front_kernel(
     width, tok_ref, wbc_ref, wdt_ref, alog_ref, bias_ref, x_ref, g_ref,
-    fresh_ref, entry_ref, proj_ref, cum_ref, rate_ref, sigcum_ref, sig_ref, dproj_ref, ra_ref, rb_ref,
-    whi, wlo, cols, rows, score, dscore,
+    fresh_ref, entry_ref, decay_ref, proj_ref, cum_ref, rate_ref, sigcum_ref, sig_ref, whi, wlo,
 ):
     k = pl.program_id(0)
     length, heads = cum_ref.shape
     half = proj_ref.shape[1] // 2
-    blocks = length // GROUP
-    pairs = [(i, j) for i in range(blocks) for j in range(i + 1)]
 
     @pl.when(k == 0)
     def _():
         tok = tok_ref[...]
-        proj = mm(tok, wbc_ref[...])
-        proj_ref[...] = proj
+        proj_ref[...] = mm(tok, wbc_ref[...])
         z = mm(tok, wdt_ref[...], NT) + bias_ref[...]
         tail = jnp.exp(-jnp.abs(z))
         rate = jnp.maximum(z, 0.0) + jnp.log1p(tail)
@@ -72,99 +68,37 @@
             >= lax.broadcasted_iota(jnp.int32, (length, length), 1)
         ).astype(F32)
         cum = exact(tri, -rate * speed)
-        sigcum = exact(tri, -sig * speed)
         cum_ref[...] = cum
         rate_ref[...] = rate
         sig_ref[...] = sig
-        sigcum_ref[...] = sigcum
+        sigcum_ref[...] = exact(tri, -sig * speed)
         for n, w in enumerate((jnp.exp(cum), jnp.exp(cum[length - 1 :] - cum) * rate)):
             hi, lo = halves(w)
             whi[n] = hi
             wlo[n] = lo
-        hi, lo = halves(cum)
-        cols[0] = hi
-        cols[1] = lo
-        cols[2] = (cum - hi.astype(F32) - lo.astype(F32)).astype(BF16)
-        hi, lo = halves(sigcum)
-        cols[3] = hi
-        cols[4] = lo
-        for n, w in enumerate((cum, rate, sigcum, sig)):
-            rows[n] = w.T
-        b, c = proj[:, :half], proj[:, half:]
-        for n, (i, j) in enumerate(pairs):
-            score[n] = exact(
-                c[i * GROUP : (i + 1) * GROUP], b[j * GROUP : (j + 1) * GROUP], NT
-            )
-        dscore[...] = jnp.zeros_like(dscore)
 
     lanes = x_ref.shape[1]
-    group = lanes // width
-    first = k * group
-    xs = x_ref[...]
-    gs = g_ref[...]
-    hot = spread(heads, lanes, width, first)
+    hot = spread(heads, lanes, width, k * (lanes // width))
     grow = mm(whi[0], hot) + mm(wlo[0], hot)
     fade = mm(whi[1], hot) + mm(wlo[1], hot)
+    decay_ref[0] = grow[length - 1 :]
     proj = proj_ref[...]
-    fresh_ref[0] = mm3(halves(proj[:, :half]), halves(fade * xs.astype(F32)), TN)
-    entry_ref[0] = mm3(halves(proj[:, half:]), halves(grow * gs.astype(F32)), TN)
-    causal = lax.broadcasted_iota(jnp.int32, (GROUP, GROUP), 0) >= lax.broadcasted_iota(
-        jnp.int32, (GROUP, GROUP), 1
-    )
-    lane_head = lax.broadcasted_iota(jnp.int32, (GROUP, lanes), 1) // width
-    for one in range(group):
-        head = first + one
-        pick = spread(heads, GROUP, GROUP, head)
-        cum_col = mm(cols[0], pick) + (mm(cols[1], pick) + mm(cols[2], pick))
-        sig_col = mm(cols[3], pick) + mm(cols[4], pick)
-        at = pl.ds(head, 1)
-        cum_row, rate_row, sc_row, sig_row = (rows[n, at, :] for n in range(4))
-        ra = jnp.zeros((1, GROUP), F32)
-        rb = jnp.zeros((1, GROUP), F32)
-        lo_lane = (one * width) // GROUP * GROUP
-        span = max(GROUP, width)
-        gh = jnp.where(
-            lane_head[:, lo_lane : lo_lane + span] == one, 1.0, 0.0
-        ).astype(BF16)
-        for n, (i, j) in enumerate(pairs):
-            ti = slice(i * GROUP, (i + 1) * GROUP)
-            sj = slice(j * GROUP, (j + 1) * GROUP)
-            gap = cum_col[ti] - cum_row[:, sj]
-            if i == j:
-                gap = jnp.where(causal, gap, -1e30)
-            inner = mm(
-                gs[ti, lo_lane : lo_lane + span] * gh, xs[sj, lo_lane : lo_lane + span], NT
-            )
-            mixed = jnp.exp(gap) * inner
-            dscore[n] += mixed * rate_row[:, sj]
-            q = score[n] * mixed
-            c0 = jnp.sum(q, axis=0, keepdims=True)
-            if i == j:
-                gap = jnp.where(causal, gap, 0.0)
-            c1 = jnp.sum(q * gap, axis=0, keepdims=True)
-            c2 = jnp.sum(q * sig_col[ti], axis=0, keepdims=True)
-            ra += rate_row[:, sj] * c1
-            rb += rate_row[:, sj] * (c2 - sc_row[:, sj] * c0) + sig_row[:, sj] * c0
-        ra_ref[at, :] = ra
-        rb_ref[at, :] = rb
-
-    @pl.when(k == pl.num_programs(0) - 1)
-    def _():
-        proj = proj_ref[...]
-        b, c = proj[:, :half], proj[:, half:]
-        dproj_ref[...] = jnp.zeros_like(dproj_ref)
-        for n, (i, j) in enumerate(pairs):
-            ti = slice(i * GROUP, (i + 1) * GROUP)
-            sj = slice(j * GROUP, (j + 1) * GROUP)
-            d = halves(dscore[n])
-            dproj_ref[ti, half:] += mm3(d, halves(b[sj]))
-            dproj_ref[sj, :half] += mm3(d, halves(c[ti]), TN)
-
-
-def chain_kernel(count, decay_ref, fresh_ref, entry_ref, state_ref, back_ref,
-                 got_f, got_b, out_f, out_b, send_f, recv_f, send_b, recv_b):
+    fresh_ref[0] = mm3(halves(proj[:, :half]), halves(fade * x_ref[...].astype(F32)), TN)
+    entry_ref[0] = mm3(halves(proj[:, half:]), halves(grow * g_ref[...].astype(F32)), TN)
+
+
+def chain_kernel(
+    count, width, decay_ref, fresh_ref, entry_ref, x_ref, g_ref,
+    proj_ref, cum_ref, rate_ref, sigcum_ref, sig_ref, out_ref, heads_ref,
+    got_f, got_b, out_f, out_b, whi, wlo, he, hf, gacc, acc, cols, rows, score, dscore,
+    ra_ref, rb_ref, send_f, recv_f, send_b, recv_b,
+):
     me = lax.axis_index("seq")
-    chunks = fresh_ref.shape[0]
+    chunks, half, lanes = fresh_ref.shape
+    length, heads = cum_ref.shape
+    blocks = length // GROUP
+    pairs = [(i, j) for i in range(blocks) for j in range(i + 1)]
+    group = lanes // width
     right = lax.rem(me + 1, count)
     left = lax.rem(me + count - 1, count)
     barrier = pltpu.get_barrier_semaphore()
@@ -172,22 +106,104 @@
         pl.semaphore_signal(
             barrier, inc=1, device_id={"seq": peer}, device_id_type=pl.DeviceIdType.MESH
         )
+
+    proj = proj_ref[...]
+    b, c = proj[:, :half], proj[:, half:]
+    cum = cum_ref[...]
+    for n, w in enumerate((jnp.exp(cum), jnp.exp(cum[length - 1 :] - cum) * rate_ref[...])):
+        hi, lo = halves(w)
+        whi[n] = hi
+        wlo[n] = lo
+    hi, lo = halves(cum)
+    cols[0] = hi
+    cols[1] = lo
+    cols[2] = (cum - hi.astype(F32) - lo.astype(F32)).astype(BF16)
+    hi, lo = halves(sigcum_ref[...])
+    cols[3] = hi
+    cols[4] = lo
+    for n, w in enumerate((cum_ref, rate_ref, sigcum_ref, sig_ref)):
+        rows[n] = w[...].T
+    for n, (i, j) in enumerate(pairs):
+        score[n] = exact(c[i * GROUP : (i + 1) * GROUP], b[j * GROUP : (j + 1) * GROUP], NT)
+    dscore[...] = jnp.zeros_like(dscore)
+    he[...] = jnp.zeros_like(he)
+    hf[...] = jnp.zeros_like(hf)
+    gacc[...] = jnp.zeros_like(gacc)
+    acc[...] = jnp.zeros_like(acc)
     pl.semaphore_wait(barrier, 2)
 
     def forward(k):
-        return pltpu.make_async_remote_copy(
-            src_ref=out_f.at[k], dst_ref=got_f.at[k], send_sem=send_f.at[k],
-            recv_sem=recv_f.at[k], device_id={"seq": right},
-            device_id_type=pl.DeviceIdType.MESH,
+        return remote(out_f.at[k], got_f.at[k], send_f.at[k], recv_f.at[k], "seq", right)
+
+    def backward(k):
+        return remote(out_b.at[k], got_b.at[k], send_b.at[k], recv_b.at[k], "seq", left)
+
+    def columns(k):
+        return pl.ds(pl.multiple_of(k * lanes, lanes), lanes)
+
+    def inner_terms(k):
+        xs = x_ref[:, columns(k)]
+        gs = g_ref[:, columns(k)]
+        causal = lax.broadcasted_iota(jnp.int32, (GROUP, GROUP), 0) >= lax.broadcasted_iota(
+            jnp.int32, (GROUP, GROUP), 1
         )
-
-    def backward(k):
-        return pltpu.make_async_remote_copy(
-            src_ref=out_b.at[k], dst_ref=got_b.at[k], send_sem=send_b.at[k],
-            recv_sem=recv_b.at[k], device_id={"seq": left},
-            device_id_type=pl.DeviceIdType.MESH,
-        )
-
+        lane_head = lax.broadcasted_iota(jnp.int32, (GROUP, lanes), 1) // width
+        span = max(GROUP, width)
+        for one in range(group):
+            head = k * group + one
+            pick = spread(heads, GROUP, GROUP, head)
+            cum_col = mm(cols[0], pick) + (mm(cols[1], pick) + mm(cols[2], pick))
+            sig_col = mm(cols[3], pick) + mm(cols[4], pick)
+            at = pl.ds(head, 1)
+            cum_row, rate_row, sc_row, sig_row = (rows[n, at, :] for n in range(4))
+            ra = jnp.zeros((1, GROUP), F32)
+            rb = jnp.zeros((1, GROUP), F32)
+            low = (one * width) // GROUP * GROUP
+            own = jnp.where(lane_head[:, low : low + span] == one, 1.0, 0.0).astype(BF16)
+            for n, (i, j) in enumerate(pairs):
+                ti = slice(i * GROUP, (i + 1) * GROUP)
+                sj = slice(j * GROUP, (j + 1) * GROUP)
+                gap = cum_col[ti] - cum_row[:, sj]
+                if i == j:
+                    gap = jnp.where(causal, gap, -1e30)
+                inner = mm(gs[ti, low : low + span] * own, xs[sj, low : low + span], NT)
+                mixed = jnp.exp(gap) * inner
+                dscore[n] += mixed * rate_row[:, sj]
+                q = score[n] * mixed
+                c0 = jnp.sum(q, axis=0, keepdims=True)
+                if i == j:
+                    gap = jnp.where(causal, gap, 0.0)
+                c1 = jnp.sum(q * gap, axis=0, keepdims=True)
+                c2 = jnp.sum(q * sig_col[ti], axis=0, keepdims=True)
+                ra += rate_row[:, sj] * c1
+                rb += rate_row[:, sj] * (c2 - sc_row[:, sj] * c0) + sig_row[:, sj] * c0
+            ra_ref[at, :] = ra
+            rb_ref[at, :] = rb
+
+    def outer_terms(k):
+        hot = spread(heads, lanes, width, k * group)
+        cold = gathers(heads, lanes, width, k * group)
+        xf = x_ref[:, columns(k)].astype(F32)
+        gf = g_ref[:, columns(k)].astype(F32)
+        state = got_f[k]
+        back = got_b[k]
+        state2 = halves(state)
+        back2 = halves(back)
+        proj = proj_ref[...]
+        grow = mm(whi[0], hot) + mm(wlo[0], hot)
+        fade = mm(whi[1], hot) + mm(wlo[1], hot)
+        hi, lo = halves(gf * mm3(halves(proj[:, half:]), state2))
+        he[...] += mm(hi, cold) + mm(lo, cold)
+        hi, lo = halves(xf * mm3(halves(proj[:, :half]), back2))
+        hf[...] += mm(hi, cold) + mm(lo, cold)
+        acc[:, half:] += mm3(halves(grow * gf), state2, NT)
+        acc[:, :half] += mm3(halves(fade * xf), back2, NT)
+        both = jnp.broadcast_to(jnp.sum(state * back, axis=0, keepdims=True), (8, lanes))
+        hi, lo = halves(both)
+        gacc[...] += mm(hi, cold) + mm(lo, cold)
+
+    lead = skew(count - 1)
+    each = pl.cdiv(chunks, lead)
     ahead = skew(me)
     behind = skew(count - 1 - me)
 
@@ -198,15 +214,16 @@
         def _():
             @pl.when(me == 0)
             def _():
-                state_ref[k] = jnp.zeros(state_ref.shape[1:], F32)
+                got_f[k] = jnp.zeros((half, lanes), F32)
                 out_f[k] = fresh_ref[k]
 
             @pl.when(me > 0)
             def _():
                 forward(k).wait_recv()
-                value = got_f[k]
-                state_ref[k] = value
-                out_f[k] = decay_ref[k] * value + fresh_ref[k]
+
+                @pl.when(me < count - 1)
+                def _():
+                    out_f[k] = decay_ref[k] * got_f[k] + fresh_ref[k]
 
             @pl.when(me < count - 1)
             def _():
@@ -218,23 +235,60 @@
         def _():
             @pl.when(me == count - 1)
             def _():
-                back_ref[j] = jnp.zeros(back_ref.shape[1:], F32)
+                got_b[j] = jnp.zeros((half, lanes), F32)
                 out_b[j] = entry_ref[j]
 
             @pl.when(me < count - 1)
             def _():
                 backward(j).wait_recv()
-                value = got_b[j]
-                back_ref[j] = value
-                out_b[j] = decay_ref[j] * value + entry_ref[j]
+
+                @pl.when(me > 0)
+                def _():
+                    out_b[j] = decay_ref[j] * got_b[j] + entry_ref[j]
 
             @pl.when(me > 0)
             def _():
                 backward(j).start()
 
+        @pl.when(tau < lead)
+        def _():
+            for n in range(each):
+                item = tau * each + n
+
+                @pl.when(item < chunks)
+                def _():
+                    inner_terms(item)
+
+        @pl.when(tau >= lead)
+        def _():
+            outer_terms(tau - lead)
+
         return unused
 
-    lax.fori_loop(0, chunks + 3 * ((count - 1) // 2) + (count - 1) % 2, step, 0)
+    lax.fori_loop(0, chunks + lead, step, 0)
+
+    for n, (i, j) in enumerate(pairs):
+        ti = slice(i * GROUP, (i + 1) * GROUP)
+        sj = slice(j * GROUP, (j + 1) * GROUP)
+        d = halves(dscore[n])
+        acc[ti, half:] += mm3(d, halves(b[sj]))
+        acc[sj, :half] += mm3(d, halves(c[ti]), TN)
+    out_ref[...] = acc[...].astype(BF16)
+    sigcum = sigcum_ref[...]
+    last = cum[length - 1 :]
+    sig_last = sigcum[length - 1 :]
+    e = jnp.exp(cum) * he[...]
+    f0 = jnp.exp(last - cum) * hf[...]
+    f = f0 * rate_ref[...]
+    link = jnp.exp(last) * gacc[0:1, :]
+    ga = jnp.sum(e * cum + f * (last - cum), axis=0, keepdims=True) + link * last
+    gb = (
+        jnp.sum(e * sigcum + f * (sig_last - sigcum) + f0 * sig_ref[...], axis=0, keepdims=True)
+        + link * sig_last
+    )
+    heads_ref[...] = jnp.zeros_like(heads_ref)
+    heads_ref[0:1, :heads] = ga + jnp.sum(ra_ref[...].T, axis=0, keepdims=True)
+    heads_ref[1:2, :heads] = gb + jnp.sum(rb_ref[...].T, axis=0, keepdims=True)
 
     def drain(k, unused):
         @pl.when(me < count - 1)
@@ -248,69 +302,6 @@
         return unused
 
     lax.fori_loop(0, chunks, drain, 0)
-
-
-def back_kernel(
-    width, x_ref, g_ref, state_ref, back_ref, proj_ref, cum_ref, rate_ref, sigcum_ref, sig_ref,
-    dproj_ref, ra_ref, rb_ref, out_ref, heads_ref, whi, wlo, he, hf, gacc, acc,
-):
-    k = pl.program_id(0)
-    length, heads = cum_ref.shape
-    half = proj_ref.shape[1] // 2
-
-    @pl.when(k == 0)
-    def _():
-        cum = cum_ref[...]
-        for n, w in enumerate((jnp.exp(cum), jnp.exp(cum[length - 1 :] - cum) * rate_ref[...])):
-            hi, lo = halves(w)
-            whi[n] = hi
-            wlo[n] = lo
-        he[...] = jnp.zeros_like(he)
-        hf[...] = jnp.zeros_like(hf)
-        gacc[...] = jnp.zeros_like(gacc)
-        acc[...] = dproj_ref[...]
-
-    lanes = x_ref.shape[1]
-    first = k * (lanes // width)
-    hot = spread(heads, lanes, width, first)
-    cold = gathers(heads, lanes, width, first)
-    xf = x_ref[...].astype(F32)
-    gf = g_ref[...].astype(F32)
-    state = state_ref[0]
-    back = back_ref[0]
-    state2 = halves(state)
-    back2 = halves(back)
-    proj = proj_ref[...]
-    grow = mm(whi[0], hot) + mm(wlo[0], hot)
-    fade = mm(whi[1], hot) + mm(wlo[1], hot)
-    hi, lo = halves(gf * mm3(halves(proj[:, half:]), state2))
-    he[...] += mm(hi, cold) + mm(lo, cold)
-    hi, lo = halves(xf * mm3(halves(proj[:, :half]), back2))
-    hf[...] += mm(hi, cold) + mm(lo, cold)
-    acc[:, half:] += mm3(halves(grow * gf), state2, NT)
-    acc[:, :half] += mm3(halves(fade * xf), back2, NT)
-    both = jnp.broadcast_to(jnp.sum(state * back, axis=0, keepdims=True), (8, lanes))
-    hi, lo = halves(both)
-    gacc[...] += mm(hi, cold) + mm(lo, cold)
-
-    @pl.when(k == pl.num_programs(0) - 1)
-    def _():
-        cum = cum_ref[...]
-        sigcum = sigcum_ref[...]
-        last = cum[length - 1 :]
-        sig_last = sigcum[length - 1 :]
-        e = jnp.exp(cum) * he[...]
-        f0 = jnp.exp(last - cum) * hf[...]
-        f = f0 * rate_ref[...]
-        link = jnp.exp(last) * gacc[0:1, :]
-        ga = jnp.sum(e * cum + f * (last - cum), axis=0, keepdims=True) + link * last
-        gb = (
-            jnp.sum(e * sigcum + f * (sig_last - sigcum) + f0 * sig_ref[...], axis=0, keepdims=True)
-            + link * sig_last
-        )
-        heads_ref[0:1, :] = ga + jnp.sum(ra_ref[...].T, axis=0, keepdims=True)
-        heads_ref[1:2, :] = gb + jnp.sum(rb_ref[...].T, axis=0, keepdims=True)
-        out_ref[...] = acc[...].astype(BF16)
 
 
 def remote(src, dst, send, recv, axis, peer):
@@ -499,59 +490,47 @@
     chunk3 = pl.BlockSpec((1, half, LANES), lambda k: (k, 0, 0))
     small = sds((length, heads), F32)
     states = sds((chunks, half, LANES), F32)
-    outs = [states, states, sds((length, wide), F32), small, small, small, small,
-            sds((length, wide), F32), sds((heads, GROUP), F32), sds((heads, GROUP), F32)]
+    outs = [states, states, sds((chunks, 1, LANES), F32), sds((length, wide), F32)] + [small] * 4
     alog2 = a_log[None]
     bias2 = dt_bias[None]
     wdt = w_dt.T
-    fresh, entry, proj, cum, rate, sigcum, sig, dproj, ra, rb = pl.pallas_call(
+    pair = pltpu.VMEM((2, length, heads), BF16)
+    fresh, entry, decay, proj, cum, rate, sigcum, sig = pl.pallas_call(
         functools.partial(front_kernel, width),
         grid=(chunks,),
         in_specs=[whole(tok), whole(w_bc), whole(wdt), whole(alog2), whole(bias2), chunk2, chunk2],
-        out_specs=[chunk3, chunk3] + [whole(o) for o in outs[2:]],
+        out_specs=[chunk3, chunk3, pl.BlockSpec((1, 1, LANES), lambda k: (k, 0, 0))]
+        + [whole(o) for o in outs[3:]],
         out_shape=outs,
-        scratch_shapes=[
-            pltpu.VMEM((2, length, heads), BF16),
-            pltpu.VMEM((2, length, heads), BF16),
-            pltpu.VMEM((5, length, heads), BF16),
-            pltpu.VMEM((4, heads, length), F32),
-            pltpu.VMEM((npairs, GROUP, GROUP), F32),
-            pltpu.VMEM((npairs, GROUP, GROUP), F32),
-        ],
+        scratch_shapes=[pair, pair],
         name="front",
     )(tok, w_bc, wdt, alog2, bias2, x, g)
-    decay = jnp.repeat(jnp.exp(cum[length - 1]), width).reshape(chunks, 1, LANES)
     vm = pl.BlockSpec(memory_space=pltpu.VMEM)
     buf = pltpu.VMEM((chunks, half, LANES), F32)
     sem = pltpu.SemaphoreType.DMA((chunks,))
-    state, back = pl.pallas_call(
-        functools.partial(chain_kernel, count),
-        in_specs=[vm, vm, vm],
+    square_tiles = pltpu.VMEM((npairs, GROUP, GROUP), F32)
+    head_rows = pltpu.VMEM((heads, GROUP), F32)
+    d_projected, grad_heads = pl.pallas_call(
+        functools.partial(chain_kernel, count, width),
+        in_specs=[vm] * 10,
         out_specs=[vm, vm],
-        out_shape=[states, states],
-        scratch_shapes=[buf, buf, buf, buf, sem, sem, sem, sem],
+        out_shape=[sds((length, wide), BF16), sds((8, GROUP), F32)],
+        scratch_shapes=[
+            buf, buf, buf, buf, pair, pair,
+            pltpu.VMEM((length, heads), F32),
+            pltpu.VMEM((length, heads), F32),
+            pltpu.VMEM((8, heads), F32),
+            pltpu.VMEM((length, wide), F32),
+            pltpu.VMEM((5, length, heads), BF16),
+            pltpu.VMEM((4, heads, length), F32),
+            square_tiles, square_tiles, head_rows, head_rows,
+            sem, sem, sem, sem,
+        ],
         compiler_params=pltpu.CompilerParams(
             collective_id=0, has_side_effects=True, vmem_limit_bytes=56 * 1024 * 1024
         ),
         name="chain",
-    )(decay, fresh, entry)
-    d_projected, grad_heads = pl.pallas_call(
-        functools.partial(back_kernel, width),
-        grid=(chunks,),
-        in_specs=[chunk2, chunk2, chunk3, chunk3]
-        + [whole(a) for a in (proj, cum, rate, sigcum, sig, dproj, ra, rb)],
-        out_specs=[whole(proj), pl.BlockSpec((2, heads), lambda k: (0, 0))],
-        out_shape=[sds((length, wide), BF16), sds((2, heads), F32)],
-        scratch_shapes=[
-            pltpu.VMEM((2, length, heads), BF16),
-            pltpu.VMEM((2, length, heads), BF16),
-            pltpu.VMEM((length, heads), F32),
-            pltpu.VMEM((length, heads), F32),
-            pltpu.VMEM((8, heads), F32),
-            pltpu.VMEM((length, wide), F32),
-        ],
-        name="back",
-    )(x, g, state, back, proj, cum, rate, sigcum, sig, dproj, ra, rb)
+    )(decay, fresh, entry, x, g, proj, cum, rate, sigcum, sig)
     own_last = last_bc[0]
     rows = own_last.shape[0]
     stages = replicas.bit_length() - 1
@@ -579,7 +558,7 @@
             collective_id=1, has_side_effects=True, vmem_limit_bytes=48 * 1024 * 1024
         ),
         name="tail",
-    )(tok, d_projected, tile(grad_heads), own_last, tile(last_heads[0]), weight)
+    )(tok, d_projected, grad_heads, own_last, tile(last_heads[0]), weight)
     summed_heads = summed[:2, :heads]
     diff_heads = summed_heads - last_heads[0]
     trigger = jnp.sqrt(jnp.sum(square[0]) + jnp.sum(diff_heads * diff_heads) + 1e-06)

time: 167 us -> 133 us (0.80)
  Pallas kernels: 156 us -> 122 us
    pallas_call x2 -> x1, Pallas kernels: 84.7 us -> 60.5 us  [local(): pl.pallas_call(functools.partial(chain_kernel, count, width), in_specs=[v...]
    pallas_call x1, Pallas kernels: 30.3 us -> 20.2 us  [local(): pl.pallas_call(functools.partial(front_kernel, width), grid=(chunks,), in...]
where the time goes in v3:
time: 133 us; the launch traced here: 131 us
  Pallas kernels  122 us (92%)
  between operations  3.87 us (3%)
  other arithmetic  3.3 us (2%)
  local copies, waits for them, and re-layouts  1.61 us (1%)
    pallas_call x1, Pallas kernels, local(): pl.pallas_call(functools.partial(chain_kernel, count, width), in_specs=[v...  60.5 us
    pallas_call x1, Pallas kernels, local(): pl.pallas_call(functools.partial(tail_kernel, count, replicas), in_specs=...  41.8 us
    pallas_call x1, Pallas kernels, local(): pl.pallas_call(functools.partial(front_kernel, width), grid=(chunks,), in...  20.2 us

profile of v3, /device:TPU:0, one launch (start us, length us, event | category | flops | bytes accessed | tf_op | source)
XLA Modules:
  0.0 131.2 jit_solution(1854547286127139280)
XLA Ops:
  0.6 20.2 %front.1 = (f32[20,128,256]{2,1,0:T(8,128)}, f32[20,128,256]{2,1,0:T(8,128)}, f32[20,1,256]{2,1,0:T(1,128)}, f32[256,256]{1,0:T(8,128)}, f32[256,80]{1,0:T(8,128...) custom-call(bf16[256,2560]{1,0:T(8,128)(2,1)} %bitcast.18, bf16[2560,256]{1,0:T(8,128)(2,1)} %wbc_ref.1, ...), custom_call_target="tpu_custom_call" | custom-call | tf_op jit(solution)/shard_map/front/pallas_call | solution.py:498
  20.8 0.0 copy-start.5
  20.8 0.0 copy-start
  20.9 0.0 copy-start.1
  20.9 0.0 copy-start.6
  20.9 0.0 copy-start.4
  20.9 60.5 %chain.1 = (bf16[256,256]{1,0:T(8,128)(2,1)}, f32[8,128]{1,0:T(8,128)}) custom-call(f32[20,1,256]{2,1,0:T(1,128)} %get-tuple-element.20.decay_ref, f32[20,128,256]{2,1,0:T(8,128)} %get-tuple-element.21.fresh_ref, f32[20,128,256]{2,1,0:T(8,128)} %get-tuple-element.22.entry_ref, bf16[256,5120]{1,0:T(8,128)(2,1)} %bitcast.22, bf16[256,5120]{1,0:T(8,128)(2,1)} %bitcast.24, ...), custom_call_target="tpu_custom_call" | custom-call | tf_op jit(solution)/shard_map/chain/pallas_call | solution.py:513
  82.0 0.0 copy-done.5
  82.1 0.0 copy-done
  82.1 0.0 copy-done.1
  82.1 0.0 copy-start.2
  82.1 0.9 copy-done.2
  83.0 0.0 copy-start.3
  83.0 0.7 copy-done.3
  83.7 41.8 %tail.1 = (f32[320,256]{1,0:T(8,128)S(1)}, f32[320,256]{1,0:T(8,128)S(1)}, f32[8,128]{1,0:T(8,128)S(1)}, f32[8,128]{1,0:T(8,128)S(1)}, f32[8,128]{1,0:T(8,128)S(1)}) custom-call(bf16[256,2560]{1,0:T(8,128)(2,1)S(1)} %bitcast.19, bf16[256,256]{1,0:T(8,128)(2,1)S(1)} %copy-done.2, f32[8,128]{1,0:T(8,128)S(1)} %copy-done.3, f32[320,256]{1,0:T(8,128)S(1)} %bitcast.20, ...), custom_call_target="tpu_custom_call" | custom-call | tf_op jit(solution)/shard_map/tail/pallas_call | solution.py:540
  125.4 0.0 copy-done.6
  125.4 1.2 multiply_reduce_fusion
  126.6 0.6 slice_reduce_fusion
  128.6 0.8 select_bitcast_fusion
  129.3 0.0 copy-done.4
  129.3 0.8 add.14
  (2 shorter events, 0.0 us)
Async XLA Ops:
  20.8 61.2 %copy-start.5 = (f32[1,2,80]{2,1,0:T(2,128)S(1)}, f32[1,2,80]{2,1,0:T(2,128)}, u32[]{:S(2)}) copy-start(f32[1,2,80]{2,1,0:T(2,128)} %param.21) | copy-start | bytes 1924
  20.8 61.2 %copy-start = (bf16[1,256,2560]{2,1,0:T(8,128)(2,1)S(1)}, bf16[1,256,2560]{2,1,0:T(8,128)(2,1)}, u32[]{:S(2)}) copy-start(bf16[1,256,2560]{2,1,0:T(8,128)(2,1)} %param.12) | copy-start | bytes 3932164
  20.9 61.2 %copy-start.1 = (f32[1,320,256]{2,1,0:T(8,128)S(1)}, f32[1,320,256]{2,1,0:T(8,128)}, u32[]{:S(2)}) copy-start(f32[1,320,256]{2,1,0:T(8,128)} %param.20) | copy-start | bytes 983044
  20.9 104.6 %copy-start.6 = (f32[2,80]{1,0:T(2,128)S(1)}, f32[2,80]{1,0:T(2,128)}, u32[]{:S(2)}) copy-start(f32[2,80]{1,0:T(2,128)} %param.23) | copy-start | bytes 1924
  20.9 108.4 %copy-start.4 = (f32[320,256]{1,0:T(8,128)S(1)}, f32[320,256]{1,0:T(8,128)}, u32[]{:S(2)}) copy-start(f32[320,256]{1,0:T(8,128)} %param.22) | copy-start | bytes 983044
  82.1 0.9 copy-start.2
  83.0 0.7 copy-start.3

commit v4 on v3

--- a/solution.py
+++ b/solution.py
@@ -34,10 +34,22 @@
     return mm(a[0], b[0], dims) + (mm(a[0], b[1], dims) + mm(a[1], b[0], dims))
 
 
-def spread(heads, lanes, per_head, first):
-    row = lax.broadcasted_iota(jnp.int32, (heads, lanes), 0)
-    lane = lax.broadcasted_iota(jnp.int32, (heads, lanes), 1)
-    return (row == first + lane // per_head).astype(F32).astype(BF16)
+def spread(heads, lanes, per_head, first, copies):
+    row = lax.broadcasted_iota(jnp.int32, (copies * heads, lanes), 0)
+    want = first + lax.broadcasted_iota(jnp.int32, (copies * heads, lanes), 1) // per_head
+    hit = row == want
+    for n in range(1, copies):
+        hit = hit | (row == want + n * heads)
+    return hit.astype(F32).astype(BF16)
+
+
+def stacked(x, copies):
+    parts = []
+    for n in range(copies):
+        part = x.astype(BF16)
+        parts.append(part.astype(F32))
+        x = x - parts[-1]
+    return jnp.concatenate(parts, axis=1).astype(BF16)
 
 
 def gathers(heads, lanes, per_head, first):
@@ -48,7 +60,7 @@
 
 def front_kernel(
     width, tok_ref, wbc_ref, wdt_ref, alog_ref, bias_ref, x_ref, g_ref,
-    fresh_ref, entry_ref, decay_ref, proj_ref, cum_ref, rate_ref, sigcum_ref, sig_ref, whi, wlo,
+    fresh_ref, entry_ref, decay_ref, proj_ref, cum_ref, rate_ref, sigcum_ref, sig_ref, w2, flipped,
 ):
     k = pl.program_id(0)
     length, heads = cum_ref.shape
@@ -57,7 +69,11 @@
     @pl.when(k == 0)
     def _():
         tok = tok_ref[...]
-        proj_ref[...] = mm(tok, wbc_ref[...])
+        proj = mm(tok, wbc_ref[...])
+        proj_ref[...] = proj
+        hi, lo = halves(proj.T)
+        flipped[0] = hi
+        flipped[1] = lo
         z = mm(tok, wdt_ref[...], NT) + bias_ref[...]
         tail = jnp.exp(-jnp.abs(z))
         rate = jnp.maximum(z, 0.0) + jnp.log1p(tail)
@@ -72,25 +88,24 @@
         rate_ref[...] = rate
         sig_ref[...] = sig
         sigcum_ref[...] = exact(tri, -sig * speed)
-        for n, w in enumerate((jnp.exp(cum), jnp.exp(cum[length - 1 :] - cum) * rate)):
-            hi, lo = halves(w)
-            whi[n] = hi
-            wlo[n] = lo
+        w2[0] = stacked(jnp.exp(cum), 2)
+        w2[1] = stacked(jnp.exp(cum[length - 1 :] - cum) * rate, 2)
 
     lanes = x_ref.shape[1]
-    hot = spread(heads, lanes, width, k * (lanes // width))
-    grow = mm(whi[0], hot) + mm(wlo[0], hot)
-    fade = mm(whi[1], hot) + mm(wlo[1], hot)
+    hot = spread(heads, lanes, width, k * (lanes // width), 2)
+    grow = mm(w2[0], hot)
+    fade = mm(w2[1], hot)
     decay_ref[0] = grow[length - 1 :]
-    proj = proj_ref[...]
-    fresh_ref[0] = mm3(halves(proj[:, :half]), halves(fade * x_ref[...].astype(F32)), TN)
-    entry_ref[0] = mm3(halves(proj[:, half:]), halves(grow * g_ref[...].astype(F32)), TN)
+    b = (flipped[0, :half, :], flipped[1, :half, :])
+    c = (flipped[0, half:, :], flipped[1, half:, :])
+    fresh_ref[0] = mm3(b, halves(fade * x_ref[...].astype(F32)))
+    entry_ref[0] = mm3(c, halves(grow * g_ref[...].astype(F32)))
 
 
 def chain_kernel(
     count, width, decay_ref, fresh_ref, entry_ref, x_ref, g_ref,
     proj_ref, cum_ref, rate_ref, sigcum_ref, sig_ref, out_ref, heads_ref,
-    got_f, got_b, out_f, out_b, whi, wlo, he, hf, gacc, acc, cols, rows, score, dscore,
+    got_f, got_b, out_f, out_b, w2, bc2, he, hf, gacc, acc, cum3, sig2, rows, score, dscore,
     ra_ref, rb_ref, send_f, recv_f, send_b, recv_b,
 ):
     me = lax.axis_index("seq")
@@ -110,17 +125,12 @@
     proj = proj_ref[...]
     b, c = proj[:, :half], proj[:, half:]
     cum = cum_ref[...]
-    for n, w in enumerate((jnp.exp(cum), jnp.exp(cum[length - 1 :] - cum) * rate_ref[...])):
-        hi, lo = halves(w)
-        whi[n] = hi
-        wlo[n] = lo
-    hi, lo = halves(cum)
-    cols[0] = hi
-    cols[1] = lo
-    cols[2] = (cum - hi.astype(F32) - lo.astype(F32)).astype(BF16)
-    hi, lo = halves(sigcum_ref[...])
-    cols[3] = hi
-    cols[4] = lo
+    w2[0] = stacked(jnp.exp(cum), 2)
+    w2[1] = stacked(jnp.exp(cum[length - 1 :] - cum) * rate_ref[...], 2)
+    bc2[0] = stacked(b, 2)
+    bc2[1] = stacked(c, 2)
+    cum3[...] = stacked(cum, 3)
+    sig2[...] = stacked(sigcum_ref[...], 2)
     for n, w in enumerate((cum_ref, rate_ref, sigcum_ref, sig_ref)):
         rows[n] = w[...].T
     for n, (i, j) in enumerate(pairs):
@@ -151,9 +161,9 @@
         span = max(GROUP, width)
         for one in range(group):
             head = k * group + one
-            pick = spread(heads, GROUP, GROUP, head)
-            cum_col = mm(cols[0], pick) + (mm(cols[1], pick) + mm(cols[2], pick))
-            sig_col = mm(cols[3], pick) + mm(cols[4], pick)
+            pick = spread(heads, GROUP, GROUP, head, 3)
+            cum_col = mm(cum3[...], pick)
+            sig_col = mm(sig2[...], pick[: 2 * heads])
             at = pl.ds(head, 1)
             cum_row, rate_row, sc_row, sig_row = (rows[n, at, :] for n in range(4))
             ra = jnp.zeros((1, GROUP), F32)
@@ -181,7 +191,7 @@
             rb_ref[at, :] = rb
 
     def outer_terms(k):
-        hot = spread(heads, lanes, width, k * group)
+        hot = spread(heads, lanes, width, k * group, 2)
         cold = gathers(heads, lanes, width, k * group)
         xf = x_ref[:, columns(k)].astype(F32)
         gf = g_ref[:, columns(k)].astype(F32)
@@ -189,12 +199,16 @@
         back = got_b[k]
         state2 = halves(state)
         back2 = halves(back)
-        proj = proj_ref[...]
-        grow = mm(whi[0], hot) + mm(wlo[0], hot)
-        fade = mm(whi[1], hot) + mm(wlo[1], hot)
-        hi, lo = halves(gf * mm3(halves(proj[:, half:]), state2))
+        grow = mm(w2[0], hot)
+        fade = mm(w2[1], hot)
+
+        def read(n, part):
+            twice = jnp.concatenate([part[0], part[0]], axis=0)
+            return mm(bc2[n], twice) + mm(bc2[n, :, :half], part[1])
+
+        hi, lo = halves(gf * read(1, state2))
         he[...] += mm(hi, cold) + mm(lo, cold)
-        hi, lo = halves(xf * mm3(halves(proj[:, :half]), back2))
+        hi, lo = halves(xf * read(0, back2))
         hf[...] += mm(hi, cold) + mm(lo, cold)
         acc[:, half:] += mm3(halves(grow * gf), state2, NT)
         acc[:, :half] += mm3(halves(fade * xf), back2, NT)
@@ -327,6 +341,8 @@
     half = rows // 2
     wide = last_ref.shape[1]
     stages = replicas.bit_length() - 1
+    parts = got_r.shape[0] // count
+    piece = rows // parts
 
     def partner(bit):
         size = 2**bit
@@ -361,13 +377,13 @@
         return remote(src, got.at[place], send.at[d], recv.at[place], "seq", place)
 
     def block(j):
-        return own.at[pl.ds(pl.multiple_of(j * rows, 8), rows)]
+        return own.at[pl.ds(pl.multiple_of(j * piece, 8), piece)]
 
     def step(tau, unused):
         t = tau - skew(me)
-        j = count - 1 - t
-
-        @pl.when((t >= 0) & (j >= me))
+        j = count * parts - 1 - t
+
+        @pl.when((t >= 0) & (j >= me * parts))
         def _():
             ref = block(j)
 
@@ -376,13 +392,13 @@
                 remote(ref, got_r.at[j], send_r.at[j], recv_r.at[j], "seq", me - 1).wait_recv()
                 ref[...] += got_r[j]
 
-            @pl.when(j > me)
+            @pl.when(j >= (me + 1) * parts)
             def _():
                 remote(ref, got_r.at[j], send_r.at[j], recv_r.at[j], "seq", me + 1).start()
 
         u = tau - skew(count - 1 - me)
 
-        @pl.when((u >= 0) & (u <= me))
+        @pl.when((u >= 0) & (u < (me + 1) * parts))
         def _():
             ref = block(u)
 
@@ -391,7 +407,7 @@
                 remote(ref, got_l.at[u], send_l.at[u], recv_l.at[u], "seq", me + 1).wait_recv()
                 ref[...] += got_l[u]
 
-            @pl.when(u < me)
+            @pl.when(u < me * parts)
             def _():
                 remote(ref, got_l.at[u], send_l.at[u], recv_l.at[u], "seq", me - 1).start()
 
@@ -399,7 +415,7 @@
 
     for d in range(1, count):
         to_peer(d, hmine, hgot, send_h, recv_h).start()
-    lax.fori_loop(0, count + skew(count - 1), step, 0)
+    lax.fori_loop(0, count * parts + skew(count - 1), step, 0)
 
     for d in range(1, count):
         from_peer(d, hmine, hgot, send_h, recv_h).wait_recv()
@@ -407,7 +423,7 @@
     for n in range(1, count):
         summed = summed + hgot[n]
     sum_ref[...] = summed
-    own_rows = block(me)[...]
+    own_rows = own[pl.ds(pl.multiple_of(me * rows, 8), rows), :]
     rows_ref[...] = own_rows
     diff = own_rows - last_ref[...]
     square = jnp.sum(diff * diff, axis=0, keepdims=True)
@@ -446,7 +462,10 @@
     total = sgot[0]
     for n in range(1, count):
         total = total + sgot[n]
-    square_ref[...] = total
+    off = summed - last_heads_ref[...]
+    line = total[0:1, :] + jnp.sum(off * off, axis=0, keepdims=True)
+    line = jnp.broadcast_to(jnp.sum(line, axis=1, keepdims=True), square_ref.shape)
+    square_ref[...] = jnp.sqrt(line + 1e-06)
 
     for s in range(stages):
         for h in range(2):
@@ -456,17 +475,17 @@
         to_peer(d, smine, sgot, send_s, recv_s).wait_send()
 
     def drain(j, unused):
-        @pl.when(j > me)
+        @pl.when(j >= (me + 1) * parts)
         def _():
             remote(block(j), got_r.at[j], send_r.at[j], recv_r.at[j], "seq", me + 1).wait_send()
 
-        @pl.when(j < me)
+        @pl.when(j < me * parts)
         def _():
             remote(block(j), got_l.at[j], send_l.at[j], recv_l.at[j], "seq", me - 1).wait_send()
 
         return unused
 
-    lax.fori_loop(0, count, drain, 0)
+    lax.fori_loop(0, count * parts, drain, 0)
 
 
 def local(
@@ -494,7 +513,7 @@
     alog2 = a_log[None]
     bias2 = dt_bias[None]
     wdt = w_dt.T
-    pair = pltpu.VMEM((2, length, heads), BF16)
+    pair = pltpu.VMEM((2, length, 2 * heads), BF16)
     fresh, entry, decay, proj, cum, rate, sigcum, sig = pl.pallas_call(
         functools.partial(front_kernel, width),
         grid=(chunks,),
@@ -502,7 +521,7 @@
         out_specs=[chunk3, chunk3, pl.BlockSpec((1, 1, LANES), lambda k: (k, 0, 0))]
         + [whole(o) for o in outs[3:]],
         out_shape=outs,
-        scratch_shapes=[pair, pair],
+        scratch_shapes=[pair, pltpu.VMEM((2, wide, length), BF16)],
         name="front",
     )(tok, w_bc, wdt, alog2, bias2, x, g)
     vm = pl.BlockSpec(memory_space=pltpu.VMEM)
@@ -516,12 +535,13 @@
         out_specs=[vm, vm],
         out_shape=[sds((length, wide), BF16), sds((8, GROUP), F32)],
         scratch_shapes=[
-            buf, buf, buf, buf, pair, pair,
+            buf, buf, buf, buf, pair, pltpu.VMEM((2, length, wide), BF16),
             pltpu.VMEM((length, heads), F32),
             pltpu.VMEM((length, heads), F32),
             pltpu.VMEM((8, heads), F32),
             pltpu.VMEM((length, wide), F32),
-            pltpu.VMEM((5, length, heads), BF16),
+            pltpu.VMEM((length, 3 * heads), BF16),
+            pltpu.VMEM((length, 2 * heads), BF16),
             pltpu.VMEM((4, heads, length), F32),
             square_tiles, square_tiles, head_rows, head_rows,
             sem, sem, sem, sem,
@@ -537,6 +557,7 @@
     tile = lambda a: jnp.pad(a, ((0, 8 - a.shape[0]), (0, GROUP - a.shape[1])))
     weight = jnp.broadcast_to(fire_flags[0].astype(F32), (8, wide))
     dma = pltpu.SemaphoreType.DMA
+    parts = 2 if rows % 16 == 0 else 1
     own_rows, fired_bc, summed, fired, square = pl.pallas_call(
         functools.partial(tail_kernel, count, replicas),
         in_specs=[vm] * 6,
@@ -544,8 +565,8 @@
         out_shape=[sds((rows, wide), F32)] * 2 + [sds((8, GROUP), F32)] * 3,
         scratch_shapes=[
             pltpu.VMEM((rows * count, wide), F32),
-            pltpu.VMEM((count, rows, wide), F32),
-            pltpu.VMEM((count, rows, wide), F32),
+            pltpu.VMEM((count * parts, rows // parts, wide), F32),
+            pltpu.VMEM((count * parts, rows // parts, wide), F32),
             pltpu.VMEM((2, stages + 1, rows // 2 + 8, wide), F32),
             pltpu.VMEM((2, stages, rows // 2 + 8, wide), F32),
             pltpu.VMEM((count, 8, GROUP), F32),
@@ -553,20 +574,18 @@
             pltpu.VMEM((count, 8, GROUP), F32),
             pltpu.VMEM((8, GROUP), F32),
         ]
-        + [dma((count,))] * 4 + [dma((2, stages))] * 2 + [dma((count,))] * 4,
+        + [dma((count * parts,))] * 4 + [dma((2, stages))] * 2 + [dma((count,))] * 4,
         compiler_params=pltpu.CompilerParams(
             collective_id=1, has_side_effects=True, vmem_limit_bytes=48 * 1024 * 1024
         ),
         name="tail",
     )(tok, d_projected, grad_heads, own_last, tile(last_heads[0]), weight)
     summed_heads = summed[:2, :heads]
-    diff_heads = summed_heads - last_heads[0]
-    trigger = jnp.sqrt(jnp.sum(square[0]) + jnp.sum(diff_heads * diff_heads) + 1e-06)
     new_total_bc = total_bc + fired_bc
     new_total_heads = total_heads + fired[:2, :heads]
     new_last_bc = jnp.where(fire_flags[0] > 0, own_rows, own_last)[None]
     new_last_heads = jnp.where(fire_flags[0] > 0, summed_heads, last_heads[0])[None]
-    return (new_total_bc, new_total_heads, new_last_bc, new_last_heads, trigger.reshape(1))
+    return (new_total_bc, new_total_heads, new_last_bc, new_last_heads, square[0, :1])
 
 
 def solution(mesh):

time: 133 us -> 122 us (0.917)
  the two profiles are of different devices: /device:TPU:0 before, /device:TPU:8 now
where the time goes in v4:
time: 122 us; the launch traced here: 121 us
  Pallas kernels  115 us (94%)
  other arithmetic  2.66 us (2%)
  local copies, waits for them, and re-layouts  2.12 us (2%)
  between operations  1.4 us (1%)
    pallas_call x1, Pallas kernels, local(): pl.pallas_call(functools.partial(chain_kernel, count, width), in_specs=[v...  55.6 us
    pallas_call x1, Pallas kernels, local(): pl.pallas_call(functools.partial(tail_kernel, count, replicas), in_specs=...  39.9 us
    pallas_call x1, Pallas kernels, local(): pl.pallas_call(functools.partial(front_kernel, width), grid=(chunks,), in...  19.7 us

profile of v4, /device:TPU:8, one launch (start us, length us, event | category | flops | bytes accessed | tf_op | source)
XLA Modules:
  0.0 121.3 jit_solution(13282005851958433779)
XLA Ops:
  0.6 19.7 %front.1 = (f32[20,128,256]{2,1,0:T(8,128)}, f32[20,128,256]{2,1,0:T(8,128)}, f32[20,1,256]{2,1,0:T(1,128)}, f32[256,256]{1,0:T(8,128)}, f32[256,80]{1,0:T(8,128...) custom-call(bf16[256,2560]{1,0:T(8,128)(2,1)} %bitcast.17, bf16[2560,256]{1,0:T(8,128)(2,1)} %wbc_ref.1, ...), custom_call_target="tpu_custom_call" | custom-call | tf_op jit(solution)/shard_map/front/pallas_call | solution.py:517
  20.3 0.0 copy-start.5
  20.3 0.0 copy-start
  20.3 0.0 copy-start.1
  20.3 0.0 copy-start.4
  20.3 55.6 %chain.1 = (bf16[256,256]{1,0:T(8,128)(2,1)}, f32[8,128]{1,0:T(8,128)}) custom-call(f32[20,1,256]{2,1,0:T(1,128)} %get-tuple-element.20.decay_ref, f32[20,128,256]{2,1,0:T(8,128)} %get-tuple-element.21.fresh_ref, f32[20,128,256]{2,1,0:T(8,128)} %get-tuple-element.22.entry_ref, bf16[256,5120]{1,0:T(8,128)(2,1)} %bitcast.21, bf16[256,5120]{1,0:T(8,128)(2,1)} %bitcast.23, ...), custom_call_target="tpu_custom_call" | custom-call | tf_op jit(solution)/shard_map/chain/pallas_call | solution.py:532
  76.0 0.0 copy-start.6
  76.7 0.0 copy-done.5
  76.7 0.0 copy-done
  76.7 0.0 copy-done.1
  76.7 0.0 copy-start.2
  76.7 0.9 copy-done.2
  77.6 0.0 copy-start.3
  77.6 0.7 copy-done.3
  78.3 39.9 %tail.1 = (f32[320,256]{1,0:T(8,128)S(1)}, f32[320,256]{1,0:T(8,128)S(1)}, f32[8,128]{1,0:T(8,128)S(1)}, f32[8,128]{1,0:T(8,128)S(1)}, f32[8,128]{1,0:T(8,128)S(1)}) custom-call(bf16[256,2560]{1,0:T(8,128)(2,1)S(1)} %bitcast.18, bf16[256,256]{1,0:T(8,128)(2,1)S(1)} %copy-done.2, f32[8,128]{1,0:T(8,128)S(1)} %copy-done.3, f32[320,256]{1,0:T(8,128)S(1)} %bitcast.19, ...), custom_call_target="tpu_custom_call" | custom-call | tf_op jit(solution)/shard_map/tail/pallas_call | solution.py:561
  118.2 0.8 select_bitcast_fusion
  118.9 0.0 copy-done.4
  118.9 0.8 add.8
  119.7 0.6 select_bitcast_fusion.1
  120.3 0.0 copy-done.6
  120.3 0.6 slice_add_fusion
  120.8 0.5 slice.11
  (2 shorter events, 0.0 us)
Async XLA Ops:
  20.3 56.4 %copy-start.5 = (f32[1,2,80]{2,1,0:T(2,128)S(1)}, f32[1,2,80]{2,1,0:T(2,128)}, u32[]{:S(2)}) copy-start(f32[1,2,80]{2,1,0:T(2,128)} %param.21) | copy-start | bytes 1924
  20.3 56.4 %copy-start = (bf16[1,256,2560]{2,1,0:T(8,128)(2,1)S(1)}, bf16[1,256,2560]{2,1,0:T(8,128)(2,1)}, u32[]{:S(2)}) copy-start(bf16[1,256,2560]{2,1,0:T(8,128)(2,1)} %param.12) | copy-start | bytes 3932164
  20.3 56.4 %copy-start.1 = (f32[1,320,256]{2,1,0:T(8,128)S(1)}, f32[1,320,256]{2,1,0:T(8,128)}, u32[]{:S(2)}) copy-start(f32[1,320,256]{2,1,0:T(8,128)} %param.20) | copy-start | bytes 983044
  20.3 98.6 %copy-start.4 = (f32[320,256]{1,0:T(8,128)S(1)}, f32[320,256]{1,0:T(8,128)}, u32[]{:S(2)}) copy-start(f32[320,256]{1,0:T(8,128)} %param.22) | copy-start | bytes 983044
  76.0 44.3 %copy-start.6 = (f32[2,80]{1,0:T(2,128)S(1)}, f32[2,80]{1,0:T(2,128)}, u32[]{:S(2)}) copy-start(f32[2,80]{1,0:T(2,128)} %param.23) | copy-start | bytes 1924
  76.7 0.9 copy-start.2
  77.6 0.7 copy-start.3

commit v5 on v4

--- a/solution.py
+++ b/solution.py
@@ -64,7 +64,6 @@
 ):
     k = pl.program_id(0)
     length, heads = cum_ref.shape
-    half = proj_ref.shape[1] // 2
 
     @pl.when(k == 0)
     def _():
@@ -91,15 +90,17 @@
         w2[0] = stacked(jnp.exp(cum), 2)
         w2[1] = stacked(jnp.exp(cum[length - 1 :] - cum) * rate, 2)
 
-    lanes = x_ref.shape[1]
-    hot = spread(heads, lanes, width, k * (lanes // width), 2)
-    grow = mm(w2[0], hot)
-    fade = mm(w2[1], hot)
-    decay_ref[0] = grow[length - 1 :]
+    per, half, lanes = fresh_ref.shape
     b = (flipped[0, :half, :], flipped[1, :half, :])
     c = (flipped[0, half:, :], flipped[1, half:, :])
-    fresh_ref[0] = mm3(b, halves(fade * x_ref[...].astype(F32)))
-    entry_ref[0] = mm3(c, halves(grow * g_ref[...].astype(F32)))
+    for n in range(per):
+        hot = spread(heads, lanes, width, (k * per + n) * (lanes // width), 2)
+        grow = mm(w2[0], hot)
+        fade = mm(w2[1], hot)
+        decay_ref[n] = grow[length - 1 :]
+        at = slice(n * lanes, (n + 1) * lanes)
+        fresh_ref[n] = mm3(b, halves(fade * x_ref[:, at].astype(F32)))
+        entry_ref[n] = mm3(c, halves(grow * g_ref[:, at].astype(F32)))
 
 
 def chain_kernel(
@@ -505,8 +506,9 @@
     npairs = blocks * (blocks + 1) // 2
     sds = jax.ShapeDtypeStruct
     whole = lambda a: pl.BlockSpec(a.shape, lambda k: (0,) * len(a.shape))
-    chunk2 = pl.BlockSpec((length, LANES), lambda k: (0, k))
-    chunk3 = pl.BlockSpec((1, half, LANES), lambda k: (k, 0, 0))
+    per = next(n for n in (4, 2, 1) if chunks % n == 0)
+    chunk2 = pl.BlockSpec((length, per * LANES), lambda k: (0, k))
+    chunk3 = pl.BlockSpec((per, half, LANES), lambda k: (k, 0, 0))
     small = sds((length, heads), F32)
     states = sds((chunks, half, LANES), F32)
     outs = [states, states, sds((chunks, 1, LANES), F32), sds((length, wide), F32)] + [small] * 4
@@ -516,9 +518,9 @@
     pair = pltpu.VMEM((2, length, 2 * heads), BF16)
     fresh, entry, decay, proj, cum, rate, sigcum, sig = pl.pallas_call(
         functools.partial(front_kernel, width),
-        grid=(chunks,),
+        grid=(chunks // per,),
         in_specs=[whole(tok), whole(w_bc), whole(wdt), whole(alog2), whole(bias2), chunk2, chunk2],
-        out_specs=[chunk3, chunk3, pl.BlockSpec((1, 1, LANES), lambda k: (k, 0, 0))]
+        out_specs=[chunk3, chunk3, pl.BlockSpec((per, 1, LANES), lambda k: (k, 0, 0))]
         + [whole(o) for o in outs[3:]],
         out_shape=outs,
         scratch_shapes=[pair, pltpu.VMEM((2, wide, length), BF16)],

time: 122 us -> 114 us (0.934)
  Pallas kernels: 115 us -> 108 us
    pallas_call x1, Pallas kernels: 19.7 us -> 12.4 us  [local(): pl.pallas_call(functools.partial(front_kernel, width), grid=(chunks // pe...]
where the time goes in v5:
time: 114 us
  Pallas kernels  108 us (95%)
  other arithmetic  2.66 us (2%)
  local copies, waits for them, and re-layouts  2.12 us (2%)
  between operations  1.41 us (1%)
    pallas_call x1, Pallas kernels, local(): pl.pallas_call(functools.partial(chain_kernel, count, width), in_specs=[v...  55.6 us
    pallas_call x1, Pallas kernels, local(): pl.pallas_call(functools.partial(tail_kernel, count, replicas), in_specs=...  39.9 us
    pallas_call x1, Pallas kernels, local(): pl.pallas_call(functools.partial(front_kernel, width), grid=(chunks // pe...  12.4 us

profile of v5, /device:TPU:8, one launch (start us, length us, event | category | flops | bytes accessed | tf_op | source)
XLA Modules:
  0.0 114.0 jit_solution(11530234777502840162)
XLA Ops:
  0.6 12.4 %front.1 = (f32[20,128,256]{2,1,0:T(8,128)}, f32[20,128,256]{2,1,0:T(8,128)}, f32[20,1,256]{2,1,0:T(1,128)}, f32[256,256]{1,0:T(8,128)}, f32[256,80]{1,0:T(8,128...) custom-call(bf16[256,2560]{1,0:T(8,128)(2,1)} %bitcast.17, bf16[2560,256]{1,0:T(8,128)(2,1)} %wbc_ref.1, ...), custom_call_target="tpu_custom_call" | custom-call | tf_op jit(solution)/shard_map/front/pallas_call | solution.py:519
  13.0 0.0 copy-start.5
  13.0 0.0 copy-start
  13.0 0.0 copy-start.1
  13.0 0.0 copy-start.4
  13.1 55.6 %chain.1 = (bf16[256,256]{1,0:T(8,128)(2,1)}, f32[8,128]{1,0:T(8,128)}) custom-call(f32[20,1,256]{2,1,0:T(1,128)} %get-tuple-element.20.decay_ref, f32[20,128,256]{2,1,0:T(8,128)} %get-tuple-element.21.fresh_ref, f32[20,128,256]{2,1,0:T(8,128)} %get-tuple-element.22.entry_ref, bf16[256,5120]{1,0:T(8,128)(2,1)} %bitcast.21, bf16[256,5120]{1,0:T(8,128)(2,1)} %bitcast.23, ...), custom_call_target="tpu_custom_call" | custom-call | tf_op jit(solution)/shard_map/chain/pallas_call | solution.py:534
  68.7 0.0 copy-start.6
  69.4 0.0 copy-done.5
  69.4 0.0 copy-done
  69.4 0.0 copy-done.1
  69.4 0.0 copy-start.2
  69.4 0.9 copy-done.2
  70.3 0.0 copy-start.3
  70.3 0.7 copy-done.3
  71.0 39.9 %tail.1 = (f32[320,256]{1,0:T(8,128)S(1)}, f32[320,256]{1,0:T(8,128)S(1)}, f32[8,128]{1,0:T(8,128)S(1)}, f32[8,128]{1,0:T(8,128)S(1)}, f32[8,128]{1,0:T(8,128)S(1)}) custom-call(bf16[256,2560]{1,0:T(8,128)(2,1)S(1)} %bitcast.18, bf16[256,256]{1,0:T(8,128)(2,1)S(1)} %copy-done.2, f32[8,128]{1,0:T(8,128)S(1)} %copy-done.3, f32[320,256]{1,0:T(8,128)S(1)} %bitcast.19, ...), custom_call_target="tpu_custom_call" | custom-call | tf_op jit(solution)/shard_map/tail/pallas_call | solution.py:563
  110.9 0.8 select_bitcast_fusion
  111.6 0.0 copy-done.4
  111.6 0.8 add.8
  112.4 0.6 select_bitcast_fusion.1
  113.0 0.0 copy-done.6
  113.0 0.6 slice_add_fusion
  113.5 0.5 slice.11
  (2 shorter events, 0.0 us)
Async XLA Ops:
  13.0 56.4 %copy-start.5 = (f32[1,2,80]{2,1,0:T(2,128)S(1)}, f32[1,2,80]{2,1,0:T(2,128)}, u32[]{:S(2)}) copy-start(f32[1,2,80]{2,1,0:T(2,128)} %param.21) | copy-start | bytes 1924
  13.0 56.4 %copy-start = (bf16[1,256,2560]{2,1,0:T(8,128)(2,1)S(1)}, bf16[1,256,2560]{2,1,0:T(8,128)(2,1)}, u32[]{:S(2)}) copy-start(bf16[1,256,2560]{2,1,0:T(8,128)(2,1)} %param.12) | copy-start | bytes 3932164
  13.0 56.4 %copy-start.1 = (f32[1,320,256]{2,1,0:T(8,128)S(1)}, f32[1,320,256]{2,1,0:T(8,128)}, u32[]{:S(2)}) copy-start(f32[1,320,256]{2,1,0:T(8,128)} %param.20) | copy-start | bytes 983044
  13.0 98.6 %copy-start.4 = (f32[320,256]{1,0:T(8,128)S(1)}, f32[320,256]{1,0:T(8,128)}, u32[]{:S(2)}) copy-start(f32[320,256]{1,0:T(8,128)} %param.22) | copy-start | bytes 983044
  68.7 44.3 %copy-start.6 = (f32[2,80]{1,0:T(2,128)S(1)}, f32[2,80]{1,0:T(2,128)}, u32[]{:S(2)}) copy-start(f32[2,80]{1,0:T(2,128)} %param.23) | copy-start | bytes 1924
  69.4 0.9 copy-start.2
  70.3 0.7 copy-start.3
